TPU v7x, 32 devices: a whole 2x2x4 slice. The times are simulated.
32 devices in a mesh: rep: 2 (over x), frame: 16 (over z, y, core).
Axes of the slice: x: 2, y: 2, z: 4, core: 2. Of those that a mesh axis runs over, the one named last changes fastest.
Arguments:
- queries: bfloat16 [12288, 1536], P(('rep', 'frame')), parts along dimension 0, may hold values from -9 to 9
- keys: bfloat16 [12288, 1536], P(('rep', 'frame')), parts along dimension 0, may hold values from -6 to 6
- values: bfloat16 [12288, 1536], P(('rep', 'frame')), parts along dimension 0, may hold values from -6 to 6
- out_grad: bfloat16 [12288, 1536], P(('rep', 'frame')), parts along dimension 0, may hold values from -6 to 6
- key_blocks: int32 [32, 18], P('rep'), parts along dimension 0, may hold values from -1 to 95, as said below
- seed_offsets: int32 [192], P(('rep', 'frame')), parts along dimension 0, may hold values from 0 to 1048575
- dropout_seed: int32 [2], P('rep'), parts along dimension 0, may hold values from 0 to 1073741823
Outputs:
- attended: bfloat16 [12288, 1536], P(('rep', 'frame')), parts along dimension 0
- query_grad: bfloat16 [12288, 1536], P(('rep', 'frame')), parts along dimension 0
- key_grad: bfloat16 [12288, 1536], P(('rep', 'frame')), parts along dimension 0
- value_grad: bfloat16 [12288, 1536], P(('rep', 'frame')), parts along dimension 0
There are 2 independent parts, one for each index of `rep`. A program takes and returns all parts, laid end to end along the dimension named above; each array names one. Nothing has to cross between parts.
Inputs may be any that keep to these rules, and one draw needn't show every extreme that they name: `key_blocks`: row r lists the key blocks read by the queries of tokens r * 384 to r * 384 + 383: first the 6 blocks of range r in order; then for each level l from 0 to 3 a window of range r - 2 ** l and then one of range r + 2 ** l, each of max(6 // 2 ** (l + 1), 1) blocks of that range consecutive modulo 6, or -1 in every entry of a window whose range lies outside the video.
All inputs are finite; a program needn't handle non-finite values.
Results may differ from a plain program's by a relative error of at most 0.0056.
Values may be sent and summed in bfloat16 or wider, within the bound.
A program may use at most 128 MiB of HBM per device.

v0:
```python
import math

import jax
import jax.numpy as jnp
from jax import lax
from jax.sharding import PartitionSpec as P

HD = 128
BLOCK = 64
LEVELS = 4


KEEP_SCALE = 1.0 / 0.9


def from_behind(value, axis, by):
    size = lax.axis_size(axis)
    pairs = [(i, i + by) for i in range(size) if 0 <= i + by < size]
    return lax.ppermute(value, axis, pairs)


def logical_right(number, amount):
    return lax.shift_right_logical(number, jnp.full_like(number, amount))


def mixing(number):
    number = number * -1640531535
    number = number ^ logical_right(number, 16)
    number = number * 739982445
    number = number ^ logical_right(number, 15)
    return number


def plan_windows(blocks_dev):
    entries = []
    slot_start = blocks_dev
    for depth_level in range(LEVELS):
        block_count = max(blocks_dev >> depth_level + 1, 1)
        distance = 2**depth_level
        entries.append((distance, slot_start, block_count))
        entries.append((-distance, slot_start + block_count, block_count))
        slot_start = slot_start + 2 * block_count
    return entries


def sender_ids(key_blocks, frame_rank, frames, blocks_dev, shift_by, slot_start, block_count):
    reader = jnp.clip(frame_rank + shift_by, 0, frames - 1)
    reader_row = lax.dynamic_slice_in_dim(key_blocks, reader, 1, 0)[0]
    listed = reader_row[slot_start : slot_start + block_count]
    return jnp.clip(listed - frame_rank * blocks_dev, 0, blocks_dev - 1)


def take_blocks(source, block_ids):
    blocks_dev = source.shape[0] // BLOCK
    shaped = source.reshape(blocks_dev, BLOCK, source.shape[1])
    return jnp.take(shaped, block_ids, axis=0).reshape(-1, source.shape[1])


def fetch_windows(keys, values, entries, id_lists, mover):
    key_list = [keys]
    value_list = [values]
    for (shift_by, slot_start, block_count), block_ids in zip(entries, id_lists):
        arrived = mover(take_blocks(keys, block_ids), take_blocks(values, block_ids), shift_by)
        key_list.append(arrived[0])
        value_list.append(arrived[1])
    return (jnp.concatenate(key_list, axis=0), jnp.concatenate(value_list, axis=0))


def head_slice(matrix, head_index):
    return lax.dynamic_slice_in_dim(matrix, head_index * HD, HD, 1)


def head_put(matrix, piece, head_index):
    return lax.dynamic_update_slice_in_dim(matrix, piece.astype(matrix.dtype), head_index * HD, 1)


def head_scores(query_part, key_part, alive_tokens, score_scale):
    raw_scores = (
        jnp.einsum("qd,kd->qk", query_part, key_part, preferred_element_type=jnp.float32)
        * score_scale
    )
    return jnp.where(alive_tokens[None, :], raw_scores, -jnp.inf)


def row_log_total(scores):
    row_top = jnp.max(scores, axis=1, keepdims=True)
    return row_top + jnp.log(jnp.sum(jnp.exp(scores - row_top), axis=1, keepdims=True))


def drop_table(row_keys, key_tokens, head_index):
    hashed = mixing(row_keys[:, None] ^ key_tokens[None, :] * 40503 + head_index * 977)
    return jnp.where(logical_right(hashed, 16) & 1023 >= 102, KEEP_SCALE, 0.0).astype(jnp.float32)


def head_gradients(weights, dropped, query_part, key_part, value_part, grad_part, score_scale):
    drop_probs = (weights * dropped).astype(jnp.bfloat16)
    grad_probs = (
        jnp.einsum("qd,kd->qk", grad_part, value_part, preferred_element_type=jnp.float32) * dropped
    )
    row_delta = jnp.sum(weights * grad_probs, axis=1, keepdims=True)
    score_grad = (weights * (grad_probs - row_delta) * score_scale).astype(jnp.bfloat16)
    query_piece = jnp.dot(score_grad, key_part, preferred_element_type=jnp.float32)
    key_piece = jnp.einsum("qk,qd->kd", score_grad, query_part, preferred_element_type=jnp.float32)
    value_piece = jnp.einsum("qk,qd->kd", drop_probs, grad_part, preferred_element_type=jnp.float32)
    return (drop_probs, query_piece, key_piece, value_piece)


def local(queries, keys, values, out_grad, key_blocks, seed_offsets, dropout_seed):
    tok_dev, row_width = queries.shape
    blocks_dev = tok_dev // BLOCK
    heads_dev = row_width // HD
    frames = lax.axis_size("frame")
    frame_rank = lax.axis_index("frame")
    score_scale = 1.0 / math.sqrt(HD)
    own_row = lax.dynamic_slice_in_dim(key_blocks, frame_rank, 1, 0)[0]
    alive_slots = own_row >= 0
    safe_ids = jnp.where(alive_slots, own_row, 0)
    key_tokens = (safe_ids[:, None] * BLOCK + jnp.arange(BLOCK, dtype=jnp.int32)[None, :]).reshape(
        -1
    )
    alive_tokens = jnp.repeat(alive_slots, BLOCK)
    query_tokens = frame_rank * tok_dev + jnp.arange(tok_dev, dtype=jnp.int32)
    row_keys = mixing(dropout_seed[0] + jnp.repeat(seed_offsets, BLOCK) + query_tokens * 7919)
    entries = plan_windows(blocks_dev)
    id_lists = [
        sender_ids(key_blocks, frame_rank, frames, blocks_dev, shift_by, slot_start, block_count)
        for shift_by, slot_start, block_count in entries
    ]

    def first_move(key_piece, value_piece, shift_by):
        return from_behind((key_piece, value_piece), "frame", shift_by)

    all_keys, all_values = fetch_windows(keys, values, entries, id_lists, first_move)
    slot_rows = all_keys.shape[0]
    zero_grads = jnp.zeros((slot_rows, row_width), jnp.float32)
    blank_rows = jnp.zeros((tok_dev, row_width), jnp.bfloat16)

    def forward_step(head_index, loop_state):
        attended, log_store = loop_state
        query_part = head_slice(queries, head_index)
        key_part = head_slice(all_keys, head_index)
        value_part = head_slice(all_values, head_index)
        scores = head_scores(query_part, key_part, alive_tokens, score_scale)
        log_total = row_log_total(scores)
        weights = jnp.exp(scores - log_total)
        drop_probs = (weights * drop_table(row_keys, key_tokens, head_index)).astype(jnp.bfloat16)
        out_piece = jnp.dot(drop_probs, value_part, preferred_element_type=jnp.float32)
        log_store = lax.dynamic_update_slice_in_dim(log_store, log_total[None], head_index, 0)
        return (head_put(attended, out_piece, head_index), log_store)

    attended, log_store = lax.fori_loop(
        0, heads_dev, forward_step, (blank_rows, jnp.zeros((heads_dev, tok_dev, 1), jnp.float32))
    )

    def second_move(key_piece, value_piece, shift_by):
        return from_behind((key_piece, value_piece), "frame", shift_by)

    again_keys, again_values = fetch_windows(keys, values, entries, id_lists, second_move)

    def backward_step(head_index, loop_state):
        query_grad, key_acc, value_acc = loop_state
        query_part = head_slice(queries, head_index)
        key_part = head_slice(again_keys, head_index)
        value_part = head_slice(again_values, head_index)
        grad_part = head_slice(out_grad, head_index)
        scores = head_scores(query_part, key_part, alive_tokens, score_scale)
        log_total = lax.dynamic_slice_in_dim(log_store, head_index, 1, 0)[0]
        weights = jnp.exp(scores - log_total)
        dropped = drop_table(row_keys, key_tokens, head_index)
        drop_probs, query_piece, key_piece, value_piece = head_gradients(
            weights, dropped, query_part, key_part, value_part, grad_part, score_scale
        )
        return (
            head_put(query_grad, query_piece, head_index),
            head_put(key_acc, key_piece, head_index),
            head_put(value_acc, value_piece, head_index),
        )

    query_grad, key_acc, value_acc = lax.fori_loop(
        0, heads_dev, backward_step, (blank_rows, zero_grads, zero_grads)
    )
    own_keys = key_acc[:tok_dev].reshape(blocks_dev, BLOCK, row_width)
    own_values = value_acc[:tok_dev].reshape(blocks_dev, BLOCK, row_width)
    for (shift_by, slot_start, block_count), block_ids in zip(entries, id_lists):
        lower_row = slot_start * BLOCK
        upper_row = (slot_start + block_count) * BLOCK
        back_keys = key_acc[lower_row:upper_row].astype(jnp.bfloat16)
        back_values = value_acc[lower_row:upper_row].astype(jnp.bfloat16)
        returned = from_behind((back_keys, back_values), "frame", -shift_by)
        own_keys = own_keys.at[block_ids].add(
            returned[0].astype(jnp.float32).reshape(block_count, BLOCK, row_width)
        )
        own_values = own_values.at[block_ids].add(
            returned[1].astype(jnp.float32).reshape(block_count, BLOCK, row_width)
        )
    key_grad = own_keys.reshape(tok_dev, row_width).astype(jnp.bfloat16)
    value_grad = own_values.reshape(tok_dev, row_width).astype(jnp.bfloat16)
    return (attended, query_grad, key_grad, value_grad)


def solution(mesh):
    return jax.shard_map(
        local,
        mesh=mesh,
        in_specs=(
            P(("rep", "frame"), None),
            P(("rep", "frame"), None),
            P(("rep", "frame"), None),
            P(("rep", "frame"), None),
            P("rep", None),
            P(("rep", "frame")),
            P("rep"),
        ),
        out_specs=(
            P(("rep", "frame"), None),
            P(("rep", "frame"), None),
            P(("rep", "frame"), None),
            P(("rep", "frame"), None),
        ),
        check_vma=False,
    )
```

profile of v0, /device:TPU:0, one launch (start us, length us, event | category | flops | bytes accessed | tf_op | source)
XLA Modules:
  0.0 417.2 jit_solution(9214465897986738868)
XLA Ops:
  7.8 3.2 collective-permute-start
  23.6 6.6 %collective-permute-start.2 = (bf16[64,1536]{1,0:T(8,128)(2,1)}, bf16[64,1536]{1,0:T(8,128)(2,1)}, u32[]{:S(2)}, u32[]{:S(2)}) collective-permute-start(bf16[64,1536]{1,0:T(8,128)(2,1)} %get-tuple-element.671), channel_id=1, source_target_pairs={{0,2},{1,3},{2,4},{3,5},{4,6},{5,7},{6,8},{7,9},{8,10},{9,11},{10,... | collective-permute-start | bytes 589832 | tf_op jit(solution)/shard_map/ppermute | solution.py:19
  31.5 2.3 collective-permute-start.8
  44.8 8.7 %collective-permute-start.4 = (bf16[64,1536]{1,0:T(8,128)(2,1)}, bf16[64,1536]{1,0:T(8,128)(2,1)S(1)}, u32[]{:S(2)}, u32[]{:S(2)}) collective-permute-start(bf16[64,1536]{1,0:T(8,128)(2,1)} %get-tuple-element.669), channel_id=1, source_target_pairs={{0,4},{1,5},{2,6},{3,7},{4,8},{5,9},{6,10},{7,11},{8,12},{9,13},{1... | collective-permute-start | bytes 589832 | tf_op jit(solution)/shard_map/ppermute | solution.py:19
  57.8 5.6 %collective-permute-start.6 = (bf16[64,1536]{1,0:T(8,128)(2,1)S(1)}, bf16[64,1536]{1,0:T(8,128)(2,1)S(1)}, u32[]{:S(2)}, u32[]{:S(2)}) collective-permute-start(bf16[64,1536]{1,0:T(8,128)(2,1)S(1)} %copy-done.19), channel_id=1, source_target_pairs={{0,8},{1,9},{2,10},{3,11},{4,12},{5,13},{6,14},{7,15},{16,24},{17,... | collective-permute-start | bytes 589832 | tf_op jit(solution)/shard_map/ppermute | solution.py:19
  72.1 7.7 %collective-permute-start.12 = (bf16[64,1536]{1,0:T(8,128)(2,1)S(1)}, bf16[64,1536]{1,0:T(8,128)(2,1)S(1)}, u32[]{:S(2)}, u32[]{:S(2)}) collective-permute-start(bf16[64,1536]{1,0:T(8,128)(2,1)S(1)} %copy-done.15), channel_id=1, source_target_pairs={{0,4},{1,5},{2,6},{3,7},{4,8},{5,9},{6,10},{7,11},{8,12},{9,13},{1... | collective-permute-start | bytes 589832 | tf_op jit(solution)/shard_map/ppermute | solution.py:19
  82.5 6.4 %collective-permute-start.14 = (bf16[64,1536]{1,0:T(8,128)(2,1)S(1)}, bf16[64,1536]{1,0:T(8,128)(2,1)S(1)}, u32[]{:S(2)}, u32[]{:S(2)}) collective-permute-start(bf16[64,1536]{1,0:T(8,128)(2,1)S(1)} %copy-done.13), channel_id=1, source_target_pairs={{0,8},{1,9},{2,10},{3,11},{4,12},{5,13},{6,14},{7,15},{16,24},{17,... | collective-permute-start | bytes 589832 | tf_op jit(solution)/shard_map/ppermute | solution.py:19
  94.3 5.8 %collective-permute-done.15 = bf16[64,1536]{1,0:T(8,128)(2,1)S(1)} collective-permute-done((bf16[64,1536]{1,0:T(8,128)(2,1)S(1)}, bf16[64,1536]{1,0:T(8,128)(2,1)S(1)}, u32[]{:S(2)}, u32[]{:S(2)}) %collective-permute-start.15) | collective-permute-done | bytes 196640 | tf_op jit(solution)/shard_map/ppermute | solution.py:19
  100.9 60.8 %while.47 = (s32[]{:T(128)}, bf16[384,1536]{1,0:T(8,128)(2,1)S(1)}, f32[12,384,1]{1,2,0:T(1,128)}, bf16[384,1536]{1,0:T(8,128)(2,1)}, bf16[1152,1536]{1,0:T(8,12...) while((s32[]{:T(128)}, bf16[384,1536]{1,0:T(8,128)(2,1)S(1)}, ...), condition=%wide.region_3.6_spmd.clone, body=%wide.region_0.5_spmd.clone.sunk | while | flops 234953088 | bytes 6147917 | solution.py:151
  162.8 3.7 broadcast_in_dim.165
  166.6 3.8 broadcast_in_dim.165.clone
  170.4 138.5 %while.48 = (s32[]{:T(128)}, bf16[384,1536]{1,0:T(8,128)(2,1)S(1)}, f32[1152,1536]{1,0:T(8,128)}, f32[1152,1536]{1,0:T(8,128)}, bf16[384,1536]{1,0:T(8,128)(2,1)...) while((s32[]{:T(128)}, bf16[384,1536]{1,0:T(8,128)(2,1)S(1)}, ...), condition=%wide.region_6.9_spmd.clone, body=%wide.region_4.8_spmd.clone.sunk | while | flops 581327232 | bytes 15878501 | solution.py:179
  179.2 2.8 convolution_dynamic-update-slice_fusion.5
  190.7 2.8 convolution_dynamic-update-slice_fusion.5
  202.2 2.8 convolution_dynamic-update-slice_fusion.5
  213.7 2.7 convolution_dynamic-update-slice_fusion.5
  223.0 2.3 convolution_dynamic-update-slice_fusion.4
  225.2 2.8 convolution_dynamic-update-slice_fusion.5
  234.5 2.3 convolution_dynamic-update-slice_fusion.4
  236.8 2.8 convolution_dynamic-update-slice_fusion.5
  248.4 2.8 convolution_dynamic-update-slice_fusion.5
  257.7 2.3 convolution_dynamic-update-slice_fusion.4
  260.0 2.8 convolution_dynamic-update-slice_fusion.5
  271.5 2.8 convolution_dynamic-update-slice_fusion.5
  283.1 2.7 convolution_dynamic-update-slice_fusion.5
  294.6 2.7 convolution_dynamic-update-slice_fusion.5
  303.9 2.3 convolution_dynamic-update-slice_fusion.4
  306.2 2.8 convolution_dynamic-update-slice_fusion.5
  308.9 3.9 convert.60
  315.3 3.1 collective-permute-start.17
  322.5 3.9 collective-permute-start.25
  327.5 3.3 slice.356
  330.9 4.6 %collective-permute-start.19 = (bf16[64,1536]{1,0:T(8,128)(2,1)}, bf16[64,1536]{1,0:T(8,128)(2,1)}, u32[]{:S(2)}, u32[]{:S(2)}) collective-permute-start(bf16[64,1536]{1,0:T(8,128)(2,1)} %get-tuple-element.656), channel_id=1, source_target_pairs={{0,2},{1,3},{2,4},{3,5},{4,6},{5,7},{6,8},{7,9},{8,10},{9,11},{10,... | collective-permute-start | bytes 589832 | tf_op jit(solution)/shard_map/ppermute | solution.py:19
  338.1 3.4 scatter_fusion
  341.5 3.5 scatter_fusion.1
  346.4 2.5 fusion.69
  348.8 13.9 %collective-permute-start.21 = (bf16[64,1536]{1,0:T(8,128)(2,1)}, bf16[64,1536]{1,0:T(8,128)(2,1)}, u32[]{:S(2)}, u32[]{:S(2)}) collective-permute-start(bf16[64,1536]{1,0:T(8,128)(2,1)} %get-tuple-element.654), channel_id=1, source_target_pairs={{0,4},{1,5},{2,6},{3,7},{4,8},{5,9},{6,10},{7,11},{8,12},{9,13},{1... | collective-permute-start | bytes 589832 | tf_op jit(solution)/shard_map/ppermute | solution.py:19
  368.7 2.3 scatter_fusion.3
  371.1 6.3 %collective-permute-start.23 = (bf16[64,1536]{1,0:T(8,128)(2,1)S(1)}, bf16[64,1536]{1,0:T(8,128)(2,1)S(1)}, u32[]{:S(2)}, u32[]{:S(2)}) collective-permute-start(bf16[64,1536]{1,0:T(8,128)(2,1)S(1)} %copy-done.6), channel_id=1, source_target_pairs={{0,8},{1,9},{2,10},{3,11},{4,12},{5,13},{6,14},{7,15},{16,24},{17,... | collective-permute-start | bytes 589832 | tf_op jit(solution)/shard_map/ppermute | solution.py:19
  379.0 3.0 collective-permute-start.27
  382.0 2.5 fusion.70
  387.2 6.7 %collective-permute-start.29 = (bf16[64,1536]{1,0:T(8,128)(2,1)S(1)}, bf16[64,1536]{1,0:T(8,128)(2,1)S(1)}, u32[]{:S(2)}, u32[]{:S(2)}) collective-permute-start(bf16[64,1536]{1,0:T(8,128)(2,1)S(1)} %copy-done.9), channel_id=1, source_target_pairs={{0,4},{1,5},{2,6},{3,7},{4,8},{5,9},{6,10},{7,11},{8,12},{9,13},{1... | collective-permute-start | bytes 589832 | tf_op jit(solution)/shard_map/ppermute | solution.py:19
  393.9 2.5 fusion.71
  398.4 5.5 %collective-permute-start.31 = (bf16[64,1536]{1,0:T(8,128)(2,1)S(1)}, bf16[64,1536]{1,0:T(8,128)(2,1)S(1)}, u32[]{:S(2)}, u32[]{:S(2)}) collective-permute-start(bf16[64,1536]{1,0:T(8,128)(2,1)S(1)} %copy-done.7), channel_id=1, source_target_pairs={{0,8},{1,9},{2,10},{3,11},{4,12},{5,13},{6,14},{7,15},{16,24},{17,... | collective-permute-start | bytes 589832 | tf_op jit(solution)/shard_map/ppermute | solution.py:19
  403.9 2.5 fusion.72
  407.0 2.4 fusion.73
  410.1 2.4 fusion.74
  412.6 2.8 convert_element_type.79
  (475 shorter events, 233.4 us)
Async XLA Ops:
  7.8 33.6 %collective-permute-start = (bf16[192,1536]{1,0:T(8,128)(2,1)}, bf16[192,1536]{1,0:T(8,128)(2,1)}, u32[]{:S(2)}, u32[]{:S(2)}) collective-permute-start(bf16[192,1536]{1,0:T(8,128)(2,1)} %bitcast.2), channel_id=1, source_target_pairs={{0,1},{1,2},{2,3},{3,4},{4,5},{5,6},{6,7},{7,8},{8,9},{9,10},{10,1... | collective-permute-start | bytes 1769480 | tf_op jit(solution)/shard_map/ppermute | solution.py:19
  13.5 18.0 %copy-start.4 = (bf16[3,64,1536]{2,1,0:T(8,128)(2,1)S(1)}, bf16[3,64,1536]{2,1,0:T(8,128)(2,1)}, u32[]{:S(2)}) copy-start(bf16[3,64,1536]{2,1,0:T(8,128)(2,1)} %get-tuple-element.684) | copy-start | bytes 1769476
  13.5 31.3 %collective-permute-start.1 = (bf16[192,1536]{1,0:T(8,128)(2,1)}, bf16[192,1536]{1,0:T(8,128)(2,1)S(1)}, u32[]{:S(2)}, u32[]{:S(2)}) collective-permute-start(bf16[192,1536]{1,0:T(8,128)(2,1)} %bitcast.4), channel_id=1, source_target_pairs={{1,0},{2,1},{3,2},{4,3},{5,4},{6,5},{7,6},{8,7},{9,8},{10,9},{11,1... | collective-permute-start | bytes 1769480 | tf_op jit(solution)/shard_map/ppermute | solution.py:19
  23.6 40.7 %collective-permute-start.2 = (bf16[64,1536]{1,0:T(8,128)(2,1)}, bf16[64,1536]{1,0:T(8,128)(2,1)}, u32[]{:S(2)}, u32[]{:S(2)}) collective-permute-start(bf16[64,1536]{1,0:T(8,128)(2,1)} %get-tuple-element.671), channel_id=1, source_target_pairs={{0,2},{1,3},{2,4},{3,5},{4,6},{5,7},{6,8},{7,9},{8,10},{9,11},{10,... | collective-permute-start | bytes 589832 | tf_op jit(solution)/shard_map/ppermute | solution.py:19
  30.2 37.0 %collective-permute-start.3 = (bf16[64,1536]{1,0:T(8,128)(2,1)}, bf16[64,1536]{1,0:T(8,128)(2,1)}, u32[]{:S(2)}, u32[]{:S(2)}) collective-permute-start(bf16[64,1536]{1,0:T(8,128)(2,1)} %get-tuple-element.670), channel_id=1, source_target_pairs={{2,0},{3,1},{4,2},{5,3},{6,4},{7,5},{8,6},{9,7},{10,8},{11,9},{12,... | collective-permute-start | bytes 589832 | tf_op jit(solution)/shard_map/ppermute | solution.py:19
  31.5 22.9 %collective-permute-start.8 = (bf16[192,1536]{1,0:T(8,128)(2,1)S(1)}, bf16[192,1536]{1,0:T(8,128)(2,1)}, u32[]{:S(2)}, u32[]{:S(2)}) collective-permute-start(bf16[192,1536]{1,0:T(8,128)(2,1)S(1)} %bitcast.155), channel_id=1, source_target_pairs={{0,1},{1,2},{2,3},{3,4},{4,5},{5,6},{6,7},{7,8},{8,9},{9,10},{10,1... | collective-permute-start | bytes 1769480 | tf_op jit(solution)/shard_map/ppermute | solution.py:19
  37.1 17.3 %copy-start.20 = (bf16[64,1536]{1,0:T(8,128)(2,1)S(1)}, bf16[64,1536]{1,0:T(8,128)(2,1)}, u32[]{:S(2)}) copy-start(bf16[64,1536]{1,0:T(8,128)(2,1)} %get-tuple-element.668) | copy-start | bytes 589828
  41.4 16.3 %copy-start.19 = (bf16[64,1536]{1,0:T(8,128)(2,1)S(1)}, bf16[64,1536]{1,0:T(8,128)(2,1)}, u32[]{:S(2)}) copy-start(bf16[64,1536]{1,0:T(8,128)(2,1)} %get-tuple-element.667) | copy-start | bytes 589828
  41.4 16.3 %collective-permute-start.9 = (bf16[192,1536]{1,0:T(8,128)(2,1)S(1)}, bf16[192,1536]{1,0:T(8,128)(2,1)S(1)}, u32[]{:S(2)}, u32[]{:S(2)}) collective-permute-start(bf16[192,1536]{1,0:T(8,128)(2,1)S(1)} %bitcast.156), channel_id=1, source_target_pairs={{1,0},{2,1},{3,2},{4,3},{5,4},{6,5},{7,6},{8,7},{9,8},{10,9},{11,1... | collective-permute-start | bytes 1769480 | tf_op jit(solution)/shard_map/ppermute | solution.py:19
  44.8 19.5 %copy-start.17 = (bf16[64,1536]{1,0:T(8,128)(2,1)S(1)}, bf16[64,1536]{1,0:T(8,128)(2,1)}, u32[]{:S(2)}) copy-start(bf16[64,1536]{1,0:T(8,128)(2,1)} %get-tuple-element.666) | copy-start | bytes 589828
  44.8 22.4 %copy-start.18 = (bf16[64,1536]{1,0:T(8,128)(2,1)S(1)}, bf16[64,1536]{1,0:T(8,128)(2,1)}, u32[]{:S(2)}) copy-start(bf16[64,1536]{1,0:T(8,128)(2,1)} %get-tuple-element.665) | copy-start | bytes 589828
  44.8 25.3 %collective-permute-start.4 = (bf16[64,1536]{1,0:T(8,128)(2,1)}, bf16[64,1536]{1,0:T(8,128)(2,1)S(1)}, u32[]{:S(2)}, u32[]{:S(2)}) collective-permute-start(bf16[64,1536]{1,0:T(8,128)(2,1)} %get-tuple-element.669), channel_id=1, source_target_pairs={{0,4},{1,5},{2,6},{3,7},{4,8},{5,9},{6,10},{7,11},{8,12},{9,13},{1... | collective-permute-start | bytes 589832 | tf_op jit(solution)/shard_map/ppermute | solution.py:19
  54.3 15.7 %copy-start.16 = (bf16[64,1536]{1,0:T(8,128)(2,1)S(1)}, bf16[64,1536]{1,0:T(8,128)(2,1)}, u32[]{:S(2)}) copy-start(bf16[64,1536]{1,0:T(8,128)(2,1)} %get-tuple-element.664) | copy-start | bytes 589828
  54.4 17.7 %copy-start.15 = (bf16[64,1536]{1,0:T(8,128)(2,1)S(1)}, bf16[64,1536]{1,0:T(8,128)(2,1)}, u32[]{:S(2)}) copy-start(bf16[64,1536]{1,0:T(8,128)(2,1)} %get-tuple-element.663) | copy-start | bytes 589828
  54.4 26.1 %copy-start.14 = (bf16[64,1536]{1,0:T(8,128)(2,1)S(1)}, bf16[64,1536]{1,0:T(8,128)(2,1)}, u32[]{:S(2)}) copy-start(bf16[64,1536]{1,0:T(8,128)(2,1)} %get-tuple-element.662) | copy-start | bytes 589828
  54.4 17.7 %collective-permute-start.5 = (bf16[64,1536]{1,0:T(8,128)(2,1)S(1)}, bf16[64,1536]{1,0:T(8,128)(2,1)S(1)}, u32[]{:S(2)}, u32[]{:S(2)}) collective-permute-start(bf16[64,1536]{1,0:T(8,128)(2,1)S(1)} %copy-done.20), channel_id=1, source_target_pairs={{4,0},{5,1},{6,2},{7,3},{8,4},{9,5},{10,6},{11,7},{12,8},{13,9},{1... | collective-permute-start | bytes 589832 | tf_op jit(solution)/shard_map/ppermute | solution.py:19
  57.7 24.7 %copy-start.13 = (bf16[64,1536]{1,0:T(8,128)(2,1)S(1)}, bf16[64,1536]{1,0:T(8,128)(2,1)}, u32[]{:S(2)}) copy-start(bf16[64,1536]{1,0:T(8,128)(2,1)} %get-tuple-element.661) | copy-start | bytes 589828
  57.7 31.8 %copy-start.12 = (bf16[64,1536]{1,0:T(8,128)(2,1)S(1)}, bf16[64,1536]{1,0:T(8,128)(2,1)}, u32[]{:S(2)}) copy-start(bf16[64,1536]{1,0:T(8,128)(2,1)} %get-tuple-element.660) | copy-start | bytes 589828
  57.8 22.7 %collective-permute-start.6 = (bf16[64,1536]{1,0:T(8,128)(2,1)S(1)}, bf16[64,1536]{1,0:T(8,128)(2,1)S(1)}, u32[]{:S(2)}, u32[]{:S(2)}) collective-permute-start(bf16[64,1536]{1,0:T(8,128)(2,1)S(1)} %copy-done.19), channel_id=1, source_target_pairs={{0,8},{1,9},{2,10},{3,11},{4,12},{5,13},{6,14},{7,15},{16,24},{17,... | collective-permute-start | bytes 589832 | tf_op jit(solution)/shard_map/ppermute | solution.py:19
  64.3 18.2 %collective-permute-start.7 = (bf16[64,1536]{1,0:T(8,128)(2,1)S(1)}, bf16[64,1536]{1,0:T(8,128)(2,1)S(1)}, u32[]{:S(2)}, u32[]{:S(2)}) collective-permute-start(bf16[64,1536]{1,0:T(8,128)(2,1)S(1)} %copy-done.17), channel_id=1, source_target_pairs={{8,0},{9,1},{10,2},{11,3},{12,4},{13,5},{14,6},{15,7},{24,16},{25,... | collective-permute-start | bytes 589832 | tf_op jit(solution)/shard_map/ppermute | solution.py:19
  67.2 22.4 %collective-permute-start.10 = (bf16[64,1536]{1,0:T(8,128)(2,1)S(1)}, bf16[64,1536]{1,0:T(8,128)(2,1)S(1)}, u32[]{:S(2)}, u32[]{:S(2)}) collective-permute-start(bf16[64,1536]{1,0:T(8,128)(2,1)S(1)} %copy-done.18), channel_id=1, source_target_pairs={{0,2},{1,3},{2,4},{3,5},{4,6},{5,7},{6,8},{7,9},{8,10},{9,11},{10,... | collective-permute-start | bytes 589832 | tf_op jit(solution)/shard_map/ppermute | solution.py:19
  70.1 21.5 %collective-permute-start.11 = (bf16[64,1536]{1,0:T(8,128)(2,1)S(1)}, bf16[64,1536]{1,0:T(8,128)(2,1)S(1)}, u32[]{:S(2)}, u32[]{:S(2)}) collective-permute-start(bf16[64,1536]{1,0:T(8,128)(2,1)S(1)} %copy-done.16), channel_id=1, source_target_pairs={{2,0},{3,1},{4,2},{5,3},{6,4},{7,5},{8,6},{9,7},{10,8},{11,9},{12,... | collective-permute-start | bytes 589832 | tf_op jit(solution)/shard_map/ppermute | solution.py:19
  72.1 20.2 %collective-permute-start.12 = (bf16[64,1536]{1,0:T(8,128)(2,1)S(1)}, bf16[64,1536]{1,0:T(8,128)(2,1)S(1)}, u32[]{:S(2)}, u32[]{:S(2)}) collective-permute-start(bf16[64,1536]{1,0:T(8,128)(2,1)S(1)} %copy-done.15), channel_id=1, source_target_pairs={{0,4},{1,5},{2,6},{3,7},{4,8},{5,9},{6,10},{7,11},{8,12},{9,13},{1... | collective-permute-start | bytes 589832 | tf_op jit(solution)/shard_map/ppermute | solution.py:19
  80.5 12.5 %collective-permute-start.13 = (bf16[64,1536]{1,0:T(8,128)(2,1)S(1)}, bf16[64,1536]{1,0:T(8,128)(2,1)S(1)}, u32[]{:S(2)}, u32[]{:S(2)}) collective-permute-start(bf16[64,1536]{1,0:T(8,128)(2,1)S(1)} %copy-done.14), channel_id=1, source_target_pairs={{4,0},{5,1},{6,2},{7,3},{8,4},{9,5},{10,6},{11,7},{12,8},{13,9},{1... | collective-permute-start | bytes 589832 | tf_op jit(solution)/shard_map/ppermute | solution.py:19
  82.5 11.2 %collective-permute-start.14 = (bf16[64,1536]{1,0:T(8,128)(2,1)S(1)}, bf16[64,1536]{1,0:T(8,128)(2,1)S(1)}, u32[]{:S(2)}, u32[]{:S(2)}) collective-permute-start(bf16[64,1536]{1,0:T(8,128)(2,1)S(1)} %copy-done.13), channel_id=1, source_target_pairs={{0,8},{1,9},{2,10},{3,11},{4,12},{5,13},{6,14},{7,15},{16,24},{17,... | collective-permute-start | bytes 589832 | tf_op jit(solution)/shard_map/ppermute | solution.py:19
  89.6 10.6 %collective-permute-start.15 = (bf16[64,1536]{1,0:T(8,128)(2,1)S(1)}, bf16[64,1536]{1,0:T(8,128)(2,1)S(1)}, u32[]{:S(2)}, u32[]{:S(2)}) collective-permute-start(bf16[64,1536]{1,0:T(8,128)(2,1)S(1)} %copy-done.12), channel_id=1, source_target_pairs={{8,0},{9,1},{10,2},{11,3},{12,4},{13,5},{14,6},{15,7},{24,16},{25,... | collective-permute-start | bytes 589832 | tf_op jit(solution)/shard_map/ppermute | solution.py:19
  308.9 10.8 %slice-start = ((s8[7077888]{0:T(1024)(128)(4,1)}), s8[4194304]{0:T(1024)(128)(4,1)S(1)}, s32[]{:S(2)}) async-start(s8[7077888]{0:T(1024)(128)(4,1)} %bitcast.143), calls=%async_computation | async-start | bytes 8388608
  308.9 10.8 %slice-start.1 = ((s8[7077888]{0:T(1024)(128)(4,1)}), s8[2883584]{0:T(1024)(128)(4,1)S(1)}, s32[]{:S(2)}) async-start(s8[7077888]{0:T(1024)(128)(4,1)} %bitcast.143), calls=%async_computation.1 | async-start | bytes 5767168
  314.0 16.9 %collective-permute-start.16 = (bf16[192,1536]{1,0:T(8,128)(2,1)S(1)}, bf16[192,1536]{1,0:T(8,128)(2,1)S(1)}, u32[]{:S(2)}, u32[]{:S(2)}) collective-permute-start(bf16[192,1536]{1,0:T(8,128)(2,1)S(1)} %get-tuple-element.659), channel_id=1, source_target_pairs={{1,0},{2,1},{3,2},{4,3},{5,4},{6,5},{7,6},{8,7},{9,8},{10,9},{11,1... | collective-permute-start | bytes 1769480 | tf_op jit(solution)/shard_map/ppermute | solution.py:19
  315.3 20.4 %collective-permute-start.17 = (bf16[192,1536]{1,0:T(8,128)(2,1)S(1)}, bf16[192,1536]{1,0:T(8,128)(2,1)S(1)}, u32[]{:S(2)}, u32[]{:S(2)}) collective-permute-start(bf16[192,1536]{1,0:T(8,128)(2,1)S(1)} %get-tuple-element.658), channel_id=1, source_target_pairs={{0,1},{1,2},{2,3},{3,4},{4,5},{5,6},{6,7},{7,8},{8,9},{9,10},{10,1... | collective-permute-start | bytes 1769480 | tf_op jit(solution)/shard_map/ppermute | solution.py:19
  318.4 26.7 %collective-permute-start.18 = (bf16[64,1536]{1,0:T(8,128)(2,1)}, bf16[64,1536]{1,0:T(8,128)(2,1)}, u32[]{:S(2)}, u32[]{:S(2)}) collective-permute-start(bf16[64,1536]{1,0:T(8,128)(2,1)} %get-tuple-element.657), channel_id=1, source_target_pairs={{2,0},{3,1},{4,2},{5,3},{6,4},{7,5},{8,6},{9,7},{10,8},{11,9},{12,... | collective-permute-start | bytes 589832 | tf_op jit(solution)/shard_map/ppermute | solution.py:19
  321.2 27.6 %collective-permute-start.24 = (bf16[192,1536]{1,0:T(8,128)(2,1)}, bf16[192,1536]{1,0:T(8,128)(2,1)}, u32[]{:S(2)}, u32[]{:S(2)}) collective-permute-start(bf16[192,1536]{1,0:T(8,128)(2,1)} %get-tuple-element.651), channel_id=1, source_target_pairs={{1,0},{2,1},{3,2},{4,3},{5,4},{6,5},{7,6},{8,7},{9,8},{10,9},{11,1... | collective-permute-start | bytes 1769480 | tf_op jit(solution)/shard_map/ppermute | solution.py:19
  322.5 41.4 %collective-permute-start.25 = (bf16[192,1536]{1,0:T(8,128)(2,1)}, bf16[192,1536]{1,0:T(8,128)(2,1)}, u32[]{:S(2)}, u32[]{:S(2)}) collective-permute-start(bf16[192,1536]{1,0:T(8,128)(2,1)} %get-tuple-element.650), channel_id=1, source_target_pairs={{0,1},{1,2},{2,3},{3,4},{4,5},{5,6},{6,7},{7,8},{8,9},{9,10},{10,1... | collective-permute-start | bytes 1769480 | tf_op jit(solution)/shard_map/ppermute | solution.py:19
  330.9 48.1 %collective-permute-start.19 = (bf16[64,1536]{1,0:T(8,128)(2,1)}, bf16[64,1536]{1,0:T(8,128)(2,1)}, u32[]{:S(2)}, u32[]{:S(2)}) collective-permute-start(bf16[64,1536]{1,0:T(8,128)(2,1)} %get-tuple-element.656), channel_id=1, source_target_pairs={{0,2},{1,3},{2,4},{3,5},{4,6},{5,7},{6,8},{7,9},{8,10},{9,11},{10,... | collective-permute-start | bytes 589832 | tf_op jit(solution)/shard_map/ppermute | solution.py:19
  335.7 51.5 %collective-permute-start.20 = (bf16[64,1536]{1,0:T(8,128)(2,1)}, bf16[64,1536]{1,0:T(8,128)(2,1)}, u32[]{:S(2)}, u32[]{:S(2)}) collective-permute-start(bf16[64,1536]{1,0:T(8,128)(2,1)} %get-tuple-element.655), channel_id=1, source_target_pairs={{4,0},{5,1},{6,2},{7,3},{8,4},{9,5},{10,6},{11,7},{12,8},{13,9},{1... | collective-permute-start | bytes 589832 | tf_op jit(solution)/shard_map/ppermute | solution.py:19
  345.1 26.0 %collective-permute-start.26 = (bf16[64,1536]{1,0:T(8,128)(2,1)}, bf16[64,1536]{1,0:T(8,128)(2,1)}, u32[]{:S(2)}, u32[]{:S(2)}) collective-permute-start(bf16[64,1536]{1,0:T(8,128)(2,1)} %get-tuple-element.649), channel_id=1, source_target_pairs={{2,0},{3,1},{4,2},{5,3},{6,4},{7,5},{8,6},{9,7},{10,8},{11,9},{12,... | collective-permute-start | bytes 589832 | tf_op jit(solution)/shard_map/ppermute | solution.py:19
  348.8 49.6 %collective-permute-start.21 = (bf16[64,1536]{1,0:T(8,128)(2,1)}, bf16[64,1536]{1,0:T(8,128)(2,1)}, u32[]{:S(2)}, u32[]{:S(2)}) collective-permute-start(bf16[64,1536]{1,0:T(8,128)(2,1)} %get-tuple-element.654), channel_id=1, source_target_pairs={{0,4},{1,5},{2,6},{3,7},{4,8},{5,9},{6,10},{7,11},{8,12},{9,13},{1... | collective-permute-start | bytes 589832 | tf_op jit(solution)/shard_map/ppermute | solution.py:19
  364.0 43.1 %collective-permute-start.22 = (bf16[64,1536]{1,0:T(8,128)(2,1)}, bf16[64,1536]{1,0:T(8,128)(2,1)}, u32[]{:S(2)}, u32[]{:S(2)}) collective-permute-start(bf16[64,1536]{1,0:T(8,128)(2,1)} %get-tuple-element.653), channel_id=1, source_target_pairs={{8,0},{9,1},{10,2},{11,3},{12,4},{13,5},{14,6},{15,7},{24,16},{25,... | collective-permute-start | bytes 589832 | tf_op jit(solution)/shard_map/ppermute | solution.py:19
  371.0 14.2 %copy-start.10 = (bf16[64,1536]{1,0:T(8,128)(2,1)S(1)}, bf16[64,1536]{1,0:T(8,128)(2,1)}, u32[]{:S(2)}) copy-start(bf16[64,1536]{1,0:T(8,128)(2,1)} %get-tuple-element.647) | copy-start | bytes 589828
  371.0 16.1 %copy-start.9 = (bf16[64,1536]{1,0:T(8,128)(2,1)S(1)}, bf16[64,1536]{1,0:T(8,128)(2,1)}, u32[]{:S(2)}) copy-start(bf16[64,1536]{1,0:T(8,128)(2,1)} %get-tuple-element.646) | copy-start | bytes 589828
  371.1 25.3 %copy-start.8 = (bf16[64,1536]{1,0:T(8,128)(2,1)S(1)}, bf16[64,1536]{1,0:T(8,128)(2,1)}, u32[]{:S(2)}) copy-start(bf16[64,1536]{1,0:T(8,128)(2,1)} %get-tuple-element.645) | copy-start | bytes 589828
  371.1 39.0 %collective-permute-start.23 = (bf16[64,1536]{1,0:T(8,128)(2,1)S(1)}, bf16[64,1536]{1,0:T(8,128)(2,1)S(1)}, u32[]{:S(2)}, u32[]{:S(2)}) collective-permute-start(bf16[64,1536]{1,0:T(8,128)(2,1)S(1)} %copy-done.6), channel_id=1, source_target_pairs={{0,8},{1,9},{2,10},{3,11},{4,12},{5,13},{6,14},{7,15},{16,24},{17,... | collective-permute-start | bytes 589832 | tf_op jit(solution)/shard_map/ppermute | solution.py:19
  379.0 6.2 %collective-permute-start.27 = (bf16[64,1536]{1,0:T(8,128)(2,1)S(1)}, bf16[64,1536]{1,0:T(8,128)(2,1)S(1)}, u32[]{:S(2)}, u32[]{:S(2)}) collective-permute-start(bf16[64,1536]{1,0:T(8,128)(2,1)S(1)} %copy-done.11), channel_id=1, source_target_pairs={{0,2},{1,3},{2,4},{3,5},{4,6},{5,7},{6,8},{7,9},{8,10},{9,11},{10,... | collective-permute-start | bytes 589832 | tf_op jit(solution)/shard_map/ppermute | solution.py:19
  382.0 16.4 %copy-start.7 = (bf16[64,1536]{1,0:T(8,128)(2,1)S(1)}, bf16[64,1536]{1,0:T(8,128)(2,1)}, u32[]{:S(2)}) copy-start(bf16[64,1536]{1,0:T(8,128)(2,1)} %get-tuple-element.644) | copy-start | bytes 589828
  385.2 11.2 %collective-permute-start.28 = (bf16[64,1536]{1,0:T(8,128)(2,1)S(1)}, bf16[64,1536]{1,0:T(8,128)(2,1)S(1)}, u32[]{:S(2)}, u32[]{:S(2)}) collective-permute-start(bf16[64,1536]{1,0:T(8,128)(2,1)S(1)} %copy-done.10), channel_id=1, source_target_pairs={{4,0},{5,1},{6,2},{7,3},{8,4},{9,5},{10,6},{11,7},{12,8},{13,9},{1... | collective-permute-start | bytes 589832 | tf_op jit(solution)/shard_map/ppermute | solution.py:19
  387.2 19.2 %collective-permute-start.29 = (bf16[64,1536]{1,0:T(8,128)(2,1)S(1)}, bf16[64,1536]{1,0:T(8,128)(2,1)S(1)}, u32[]{:S(2)}, u32[]{:S(2)}) collective-permute-start(bf16[64,1536]{1,0:T(8,128)(2,1)S(1)} %copy-done.9), channel_id=1, source_target_pairs={{0,4},{1,5},{2,6},{3,7},{4,8},{5,9},{6,10},{7,11},{8,12},{9,13},{1... | collective-permute-start | bytes 589832 | tf_op jit(solution)/shard_map/ppermute | solution.py:19
  396.4 13.1 %collective-permute-start.30 = (bf16[64,1536]{1,0:T(8,128)(2,1)S(1)}, bf16[64,1536]{1,0:T(8,128)(2,1)S(1)}, u32[]{:S(2)}, u32[]{:S(2)}) collective-permute-start(bf16[64,1536]{1,0:T(8,128)(2,1)S(1)} %copy-done.8), channel_id=1, source_target_pairs={{8,0},{9,1},{10,2},{11,3},{12,4},{13,5},{14,6},{15,7},{24,16},{25,... | collective-permute-start | bytes 589832 | tf_op jit(solution)/shard_map/ppermute | solution.py:19
  398.4 17.0 %collective-permute-start.31 = (bf16[64,1536]{1,0:T(8,128)(2,1)S(1)}, bf16[64,1536]{1,0:T(8,128)(2,1)S(1)}, u32[]{:S(2)}, u32[]{:S(2)}) collective-permute-start(bf16[64,1536]{1,0:T(8,128)(2,1)S(1)} %copy-done.7), channel_id=1, source_target_pairs={{0,8},{1,9},{2,10},{3,11},{4,12},{5,13},{6,14},{7,15},{16,24},{17,... | collective-permute-start | bytes 589832 | tf_op jit(solution)/shard_map/ppermute | solution.py:19
  (17 other events, 83.0 us)
where the time goes:
time: 422 us; the launch traced here: 417 us
  matrix products  163 us (39%)
  starting transfers between devices  110 us (26%)
  local copies, waits for them, and re-layouts  68.1 us (16%)
  other arithmetic  63.1 us (15%)
  waiting for transfers between devices  6.54 us (2%)
  between operations  5.86 us (1%)
    ppermute x32, starting transfers between devices, from_behind(): return lax.ppermute(value, axis, pairs)  110 us
    dot_general x24, matrix products, head_scores(): jnp.einsum('qd,kd->qk', query_part, key_part, preferred_element_type=jnp....  39.7 us
    dot_general x12, matrix products, head_gradients(): jnp.einsum('qk,qd->kd', drop_probs, grad_part, preferred_element_type=jnp...  33.2 us
    dot_general x12, matrix products, head_gradients(): jnp.einsum('qk,qd->kd', score_grad, query_part, preferred_element_type=jn...  27 us
    dot_general x12, matrix products, forward_step(): jnp.dot(drop_probs, value_part, preferred_element_type=jnp.float32)  24.6 us
    dot_general x12, matrix products, head_gradients(): jnp.einsum('qd,kd->qk', grad_part, value_part, preferred_element_type=jnp...  22 us
    scatter-add x8, other arithmetic, local(): own_keys.at[block_ids]  21.7 us
    unnamed x82, local copies, waits for them, and re-layouts  17.6 us
  transfers between devices with their start and end apart: 32, of which 2 were waited for; matrix products, arithmetic and copies ran while one was open for 17% of the time, Pallas kernels for 0%

commit v1 on v0

v1 whole, which is shorter than its diff:
```python
import functools
import math

import jax
import jax.numpy as jnp
from jax import lax
from jax.experimental import pallas as pl
from jax.experimental.pallas import tpu as pltpu
from jax.sharding import PartitionSpec as P

HD = 128
BLOCK = 64
LEVELS = 4
KEEP_SCALE = 1.0 / 0.9
CHUNKS = 3
ROWS = 128


def logical_right(number, amount):
    return lax.shift_right_logical(number, jnp.full_like(number, amount))


def mixing(number):
    number = number * -1640531535
    number = number ^ logical_right(number, 16)
    number = number * 739982445
    number = number ^ logical_right(number, 15)
    return number


def plan_windows(blocks_dev):
    entries = []
    slot_start = blocks_dev
    for depth_level in range(LEVELS):
        block_count = max(blocks_dev >> depth_level + 1, 1)
        distance = 2**depth_level
        entries.append((distance, slot_start, block_count))
        entries.append((-distance, slot_start + block_count, block_count))
        slot_start = slot_start + 2 * block_count
    return entries


def shift(value, by):
    size = lax.axis_size("frame")
    pairs = [(i, i + by) for i in range(size) if 0 <= i + by < size]
    return lax.ppermute(value, "frame", pairs)


def sender_ids(key_blocks, frame_rank, frames, blocks_dev, shift_by, slot_start, block_count):
    reader = jnp.clip(frame_rank + shift_by, 0, frames - 1)
    reader_row = lax.dynamic_slice_in_dim(key_blocks, reader, 1, 0)[0]
    listed = reader_row[slot_start : slot_start + block_count]
    return jnp.clip(listed - frame_rank * blocks_dev, 0, blocks_dev - 1)


def pack_kernel(counts, ids_ref, k_ref, v_ref, *out_refs):
    at = 0
    for out_ref, count in zip(out_refs, counts):
        for j in range(count):
            start = pl.multiple_of(ids_ref[at] * BLOCK, BLOCK)
            at += 1
            rows = slice(j * BLOCK, (j + 1) * BLOCK)
            out_ref[0, rows, :] = k_ref[pl.ds(start, BLOCK), :]
            out_ref[1, rows, :] = v_ref[pl.ds(start, BLOCK), :]


def contract(a, b, dim_a, dim_b):
    return lax.dot_general(
        a, b, (((dim_a,), (dim_b,)), ((), ())), preferred_element_type=jnp.float32
    )


def fold_rows(x, op):
    total = x[0:8]
    for r in range(8, x.shape[0], 8):
        total = op(total, x[r : r + 8])
    return total


def main_kernel(spans, first_head, n_alias, *refs):
    n_win = len(spans)
    rk_ref, kt_ref, bias_ref, q_ref, k_ref, v_ref, do_ref = refs[:7]
    win_refs = refs[7 : 7 + n_win]
    outs = refs[7 + n_win + n_alias :]
    att_ref, dq_ref, own_ref = outs[:3]
    back_refs = outs[3 : 3 + n_win]
    kall, vall, s_ref, dp_ref, pd_ref, ds_ref, gk_ref, gv_ref = outs[3 + n_win :]
    tok = q_ref.shape[0]
    slots = kall.shape[0]
    score_scale = 1.0 / math.sqrt(HD)
    exp_scale = score_scale * math.log2(math.e)
    steps = slots // ROWS
    tiles = tok // 128

    kall[0:tok, :] = k_ref[...]
    vall[0:tok, :] = v_ref[...]
    for win_ref, (lo, hi) in zip(win_refs, spans):
        kall[lo:hi, :] = win_ref[0]
        vall[lo:hi, :] = win_ref[1]

    def rows_of(j):
        return pl.ds(pl.multiple_of(j * ROWS, ROWS), ROWS)

    def pass_a(j, top):
        rows = rows_of(j)
        raw = contract(kall[rows, :], q_ref[...], 1, 1)
        bias = bias_ref[rows, :]
        new_top = []
        for t in range(tiles):
            lanes = slice(t * 128, (t + 1) * 128)
            s = raw[:, lanes] + bias
            s_ref[rows, lanes] = s
            new_top.append(jnp.maximum(top[t], fold_rows(s, jnp.maximum)))
        return tuple(new_top)

    top = lax.fori_loop(
        0, steps, pass_a, tuple(jnp.full((8, 128), -jnp.inf, jnp.float32) for _ in range(tiles))
    )
    top = [jnp.max(t, axis=0, keepdims=True) for t in top]
    head_term = (first_head + pl.program_id(0)) * 977
    row_keys = [rk_ref[:, t * 128 : (t + 1) * 128] for t in range(tiles)]

    def pass_b(j, sums):
        rows = rows_of(j)
        grads = contract(vall[rows, :], do_ref[...], 1, 1)
        token_term = kt_ref[rows, :] + head_term
        new_sums = []
        for t in range(tiles):
            lanes = slice(t * 128, (t + 1) * 128)
            e = jnp.exp2((s_ref[rows, lanes] - top[t]) * exp_scale)
            x = token_term ^ row_keys[t]
            x = x * -1640531535
            x = x ^ logical_right(x, 16)
            x = x * 739982445
            x = x ^ logical_right(x, 15)
            keep = (x & (1023 << 16)) >= (102 << 16)
            dp = grads[:, lanes]
            dp_ref[rows, lanes] = dp
            s_ref[rows, lanes] = jnp.where(keep, e, -e)
            kept = jnp.where(keep, e * dp, 0.0)
            new_sums.append(sums[2 * t] + fold_rows(e, jnp.add))
            new_sums.append(sums[2 * t + 1] + fold_rows(kept, jnp.add))
        return tuple(new_sums)

    sums = lax.fori_loop(
        0, steps, pass_b, tuple(jnp.zeros((8, 128), jnp.float32) for _ in range(2 * tiles))
    )
    sums = [jnp.sum(x, axis=0, keepdims=True) for x in sums]
    inv = [KEEP_SCALE / sums[2 * t] for t in range(tiles)]
    delta = [sums[2 * t + 1] * inv[t] * (inv[t] / KEEP_SCALE) for t in range(tiles)]

    def pass_c(j, _):
        rows = rows_of(j)
        for t in range(tiles):
            lanes = slice(t * 128, (t + 1) * 128)
            es = s_ref[rows, lanes]
            pd = jnp.maximum(es, 0.0) * inv[t]
            ds = pd * dp_ref[rows, lanes] - jnp.abs(es) * delta[t]
            pd_ref[rows, lanes] = pd.astype(jnp.bfloat16)
            ds_ref[rows, lanes] = ds.astype(jnp.bfloat16)
        gk_ref[rows, :] = contract(ds_ref[rows, :], q_ref[...], 1, 0) * score_scale
        gv_ref[rows, :] = contract(pd_ref[rows, :], do_ref[...], 1, 0)
        return 0

    lax.fori_loop(0, steps, pass_c, 0)
    att_ref[...] = contract(pd_ref[...], vall[...], 0, 0).astype(jnp.bfloat16)
    dq_ref[...] = (contract(ds_ref[...], kall[...], 0, 0) * score_scale).astype(jnp.bfloat16)
    own_ref[0] = gk_ref[0:tok, :]
    own_ref[1] = gv_ref[0:tok, :]
    for back_ref, (lo, hi) in zip(back_refs, spans):
        back_ref[0] = gk_ref[lo:hi, :].astype(jnp.bfloat16)
        back_ref[1] = gv_ref[lo:hi, :].astype(jnp.bfloat16)


def finish_kernel(counts, n_alias, ids_ref, own_ref, *refs):
    ret_refs = refs[: len(counts)]
    kg_ref, vg_ref, acc = refs[len(counts) + n_alias :]
    acc[...] = own_ref[...]
    at = 0
    for ret_ref, count in zip(ret_refs, counts):
        for j in range(count):
            rows = pl.ds(pl.multiple_of(ids_ref[at] * BLOCK, BLOCK), BLOCK)
            at += 1
            acc[:, rows, :] += ret_ref[:, j * BLOCK : (j + 1) * BLOCK, :].astype(jnp.float32)
    kg_ref[...] = acc[0].astype(jnp.bfloat16)
    vg_ref[...] = acc[1].astype(jnp.bfloat16)


def local(queries, keys, values, out_grad, key_blocks, seed_offsets, dropout_seed):
    tok, width = queries.shape
    blocks_dev = tok // BLOCK
    heads = width // HD
    chunks = CHUNKS if heads % CHUNKS == 0 else 1
    nh = heads // chunks
    wc = nh * HD
    frames = lax.axis_size("frame")
    frame_rank = lax.axis_index("frame")
    entries = plan_windows(blocks_dev)
    counts = [count for _, _, count in entries]
    spans = [(start * BLOCK, (start + count) * BLOCK) for _, start, count in entries]
    slots = key_blocks.shape[1] * BLOCK
    ids = jnp.concatenate(
        [sender_ids(key_blocks, frame_rank, frames, blocks_dev, *entry) for entry in entries]
    )
    listed = lax.dynamic_slice_in_dim(key_blocks, frame_rank, 1, 0)[0]
    alive = listed >= 0
    tokens = (jnp.where(alive, listed, 0)[:, None] * BLOCK + jnp.arange(BLOCK, dtype=jnp.int32)).reshape(-1)
    token_terms = jnp.broadcast_to((tokens * 40503)[:, None], (slots, 128))
    bias = jnp.where(jnp.repeat(alive, BLOCK), 0.0, -jnp.inf).astype(jnp.float32)
    bias = jnp.broadcast_to(bias[:, None], (slots, 128))
    query_tokens = frame_rank * tok + jnp.arange(tok, dtype=jnp.int32)
    row_keys = mixing(dropout_seed[0] + jnp.repeat(seed_offsets, BLOCK) + query_tokens * 7919)[None, :]

    bf16, f32 = jnp.bfloat16, jnp.float32
    smem = pl.BlockSpec(memory_space=pltpu.SMEM)
    anyspec = pl.BlockSpec(memory_space=pl.ANY)
    win_shapes = [jax.ShapeDtypeStruct((2, n * BLOCK, wc), bf16) for n in counts]
    win_specs = [pl.BlockSpec((2, n * BLOCK, HD), lambda h: (0, 0, h)) for n in counts]
    full = jax.ShapeDtypeStruct((tok, width), bf16)

    arrived = []
    for c in range(chunks):
        column = pl.BlockSpec((tok, wc), lambda i, c=c: (0, c))
        packed = pl.pallas_call(
            functools.partial(pack_kernel, counts),
            grid=(1,),
            in_specs=[smem, column, column],
            out_specs=[pl.BlockSpec((2, n * BLOCK, wc), lambda i: (0, 0, 0)) for n in counts],
            out_shape=win_shapes,
            cost_estimate=pl.CostEstimate(flops=0, bytes_accessed=tok * wc * 12, transcendentals=0),
            name="pack",
        )(ids, keys, values)
        arrived.append([shift(p, e[0]) for p, e in zip(packed, entries)])

    outs = []
    owns = []
    returned = []
    for c in range(chunks):
        head = pl.BlockSpec((tok, HD), lambda h, c=c: (0, c * nh + h))
        n_alias = len(outs)
        n_in = 7 + len(entries)
        result = pl.pallas_call(
            functools.partial(main_kernel, spans, c * nh, n_alias),
            grid=(nh,),
            in_specs=[
                pl.BlockSpec((1, tok), lambda h: (0, 0)),
                pl.BlockSpec((slots, 128), lambda h: (0, 0)),
                pl.BlockSpec((slots, 128), lambda h: (0, 0)),
                head, head, head, head, *win_specs, *([anyspec] * n_alias),
            ],
            out_specs=[head, head, pl.BlockSpec((2, tok, HD), lambda h: (0, 0, h)), *win_specs],
            out_shape=[full, full, jax.ShapeDtypeStruct((2, tok, wc), f32), *win_shapes],
            scratch_shapes=[
                pltpu.VMEM((slots, HD), bf16),
                pltpu.VMEM((slots, HD), bf16),
                pltpu.VMEM((slots, tok), f32),
                pltpu.VMEM((slots, tok), f32),
                pltpu.VMEM((slots, tok), bf16),
                pltpu.VMEM((slots, tok), bf16),
                pltpu.VMEM((slots, HD), f32),
                pltpu.VMEM((slots, HD), f32),
            ],
            input_output_aliases={n_in + i: i for i in range(n_alias)},
            compiler_params=pltpu.CompilerParams(dimension_semantics=("arbitrary",)),
            cost_estimate=pl.CostEstimate(
                flops=nh * 12 * tok * slots * HD, bytes_accessed=nh * slots * HD * 16,
                transcendentals=nh * tok * slots,
            ),
            name="attend",
        )(row_keys, token_terms, bias, queries, keys, values, out_grad, *arrived[c], *outs)
        outs = list(result[:2])
        owns.append(result[2])
        returned.append([shift(p, -e[0]) for p, e in zip(result[3:], entries)])

    grads = []
    for c in range(chunks):
        head = pl.BlockSpec((tok, HD), lambda h, c=c: (0, c * nh + h))
        n_alias = len(grads)
        n_in = 2 + len(entries)
        grads = pl.pallas_call(
            functools.partial(finish_kernel, counts, n_alias),
            grid=(nh,),
            in_specs=[
                smem, pl.BlockSpec((2, tok, HD), lambda h: (0, 0, h)), *win_specs,
                *([anyspec] * n_alias),
            ],
            out_specs=[head, head],
            out_shape=[full, full],
            scratch_shapes=[pltpu.VMEM((2, tok, HD), f32)],
            input_output_aliases={n_in + i: i for i in range(n_alias)},
            compiler_params=pltpu.CompilerParams(dimension_semantics=("arbitrary",)),
            cost_estimate=pl.CostEstimate(
                flops=0, bytes_accessed=nh * slots * HD * 10, transcendentals=0
            ),
            name="finish",
        )(ids, owns[c], *returned[c], *grads)
    return (outs[0], outs[1], grads[0], grads[1])


def solution(mesh):
    rows = P(("rep", "frame"), None)
    return jax.shard_map(
        local,
        mesh=mesh,
        in_specs=(rows, rows, rows, rows, P("rep", None), P(("rep", "frame")), P("rep")),
        out_specs=(rows, rows, rows, rows),
        check_vma=False,
    )
```

time: 422 us -> 280 us (0.66)
  matrix products: 163 us -> 0 us
  Pallas kernels: 0 us -> 103 us
  other arithmetic: 63.1 us -> 2.1 us
  local copies, waits for them, and re-layouts: 68.1 us -> 9.89 us
  starting transfers between devices: 110 us -> 141 us
  waiting for transfers between devices: 6.54 us -> 14.9 us
    dot_general x84 -> x0, matrix products: 163 us -> none  [the longest x24 39.7 us: head_scores(): jnp.einsum('qd,kd->qk', query_part, key_part, preferred_element_type=jnp....]
    pallas_call x0 -> x9, Pallas kernels: none -> 103 us  [the longest x3 84.4 us: local(): pl.pallas_call(functools.partial(main_kernel, spans, c * nh, n_alias), gr...]
    ppermute x32 -> x48, starting transfers between devices: 110 us -> 141 us  [shift(): return lax.ppermute(value, 'frame', pairs)]
    scatter-add x16 -> x0, other arithmetic: 30.2 us -> none  [the longest x8 21.7 us: local(): own_keys.at[block_ids]]
    unnamed x82 -> x112, local copies, waits for them, and re-layouts: 17.6 us -> 2.4 us
    broadcast_in_dim x52 -> x3, local copies, waits for them, and re-layouts: 11.6 us -> 2.13 us  [the longest x1 1.03 us: local(): token_terms = jnp.broadcast_to((tokens * 40503)[:, None], (slots, 128))]
    ppermute x32 -> x48, waiting for transfers between devices: 6.54 us -> 14.9 us  [shift(): return lax.ppermute(value, 'frame', pairs)]
    dynamic_slice x12 -> x0, local copies, waits for them, and re-layouts: 8.24 us -> none  [backward_step(): log_total = lax.dynamic_slice_in_dim(log_store, head_index, 1, 0)[0]]
  transfers between devices with their start and end apart: 32 -> 48, of which waited for: 2 -> 3; matrix products, arithmetic and copies ran while one was open for 17% -> 2% of each run, Pallas kernels for 0% -> 35%
where the time goes in v1:
time: 280 us; the launch traced here: 278 us
  starting transfers between devices  141 us (50%)
  Pallas kernels  103 us (37%)
  waiting for transfers between devices  14.9 us (5%)
  local copies, waits for them, and re-layouts  9.89 us (4%)
  between operations  6.66 us (2%)
    ppermute x48, starting transfers between devices, shift(): return lax.ppermute(value, 'frame', pairs)  141 us
    pallas_call x3, Pallas kernels, local(): pl.pallas_call(functools.partial(main_kernel, spans, c * nh, n_alias), gr...  84.4 us
    ppermute x48, waiting for transfers between devices, shift(): return lax.ppermute(value, 'frame', pairs)  14.9 us
    pallas_call x3, Pallas kernels, local(): pl.pallas_call(functools.partial(finish_kernel, counts, n_alias), grid=(n...  11.8 us
    pallas_call x3, Pallas kernels, local(): pl.pallas_call(functools.partial(pack_kernel, counts), grid=(1,), in_spec...  7.27 us
  transfers between devices with their start and end apart: 48, of which 3 were waited for; matrix products, arithmetic and copies ran while one was open for 2% of the time, Pallas kernels for 35%

profile of v1, /device:TPU:0, one launch (start us, length us, event | category | flops | bytes accessed | tf_op | source)
XLA Modules:
  0.0 278.3 jit_solution(5675524806238567644)
XLA Ops:
  9.7 2.3 pack.5
  12.1 5.6 %collective-permute-start.18 = (bf16[2,64,512]{2,1,0:T(8,128)(2,1)}, bf16[2,64,512]{2,1,0:T(8,128)(2,1)}, u32[]{:S(2)}, u32[]{:S(2)}) collective-permute-start(bf16[2,64,512]{2,1,0:T(8,128)(2,1)} %get-tuple-element.85), channel_id=1, source_target_pairs={{0,2},{1,3},{2,4},{3,5},{4,6},{5,7},{6,8},{7,9},{8,10},{9,11},{10,... | collective-permute-start | bytes 393224 | tf_op jit(solution)/shard_map/ppermute | solution.py:46
  18.9 4.8 %collective-permute-start.20 = (bf16[2,64,512]{2,1,0:T(8,128)(2,1)}, bf16[2,64,512]{2,1,0:T(8,128)(2,1)S(1)}, u32[]{:S(2)}, u32[]{:S(2)}) collective-permute-start(bf16[2,64,512]{2,1,0:T(8,128)(2,1)} %get-tuple-element.87), channel_id=1, source_target_pairs={{0,4},{1,5},{2,6},{3,7},{4,8},{5,9},{6,10},{7,11},{8,12},{9,13},{1... | collective-permute-start | bytes 393224 | tf_op jit(solution)/shard_map/ppermute | solution.py:46
  23.8 1.3 collective-permute-start.21
  25.1 5.5 %collective-permute-start.22 = (bf16[2,64,512]{2,1,0:T(8,128)(2,1)}, bf16[2,64,512]{2,1,0:T(8,128)(2,1)S(1)}, u32[]{:S(2)}, u32[]{:S(2)}) collective-permute-start(bf16[2,64,512]{2,1,0:T(8,128)(2,1)} %get-tuple-element.89), channel_id=1, source_target_pairs={{0,8},{1,9},{2,10},{3,11},{4,12},{5,13},{6,14},{7,15},{16,24},{17,... | collective-permute-start | bytes 393224 | tf_op jit(solution)/shard_map/ppermute | solution.py:46
  30.6 1.3 collective-permute-start.23
  31.9 2.4 pack.4
  34.4 2.5 pack.3
  38.3 2.6 collective-permute-start.10
  43.5 6.4 %collective-permute-start.12 = (bf16[2,64,512]{2,1,0:T(8,128)(2,1)S(1)}, bf16[2,64,512]{2,1,0:T(8,128)(2,1)S(1)}, u32[]{:S(2)}, u32[]{:S(2)}) collective-permute-start(bf16[2,64,512]{2,1,0:T(8,128)(2,1)S(1)} %copy-done.52), channel_id=1, source_target_pairs={{0,4},{1,5},{2,6},{3,7},{4,8},{5,9},{6,10},{7,11},{8,12},{9,13},{1... | collective-permute-start | bytes 393224 | tf_op jit(solution)/shard_map/ppermute | solution.py:46
  50.0 1.3 collective-permute-start.13
  51.3 6.4 %collective-permute-start.14 = (bf16[2,64,512]{2,1,0:T(8,128)(2,1)S(1)}, bf16[2,64,512]{2,1,0:T(8,128)(2,1)S(1)}, u32[]{:S(2)}, u32[]{:S(2)}) collective-permute-start(bf16[2,64,512]{2,1,0:T(8,128)(2,1)S(1)} %copy-done.50), channel_id=1, source_target_pairs={{0,8},{1,9},{2,10},{3,11},{4,12},{5,13},{6,14},{7,15},{16,24},{17,... | collective-permute-start | bytes 393224 | tf_op jit(solution)/shard_map/ppermute | solution.py:46
  57.8 1.3 collective-permute-start.16
  59.2 1.3 collective-permute-start.17
  60.5 1.3 collective-permute-start.15
  61.8 5.1 %collective-permute-start.2 = (bf16[2,64,512]{2,1,0:T(8,128)(2,1)}, bf16[2,64,512]{2,1,0:T(8,128)(2,1)S(1)}, u32[]{:S(2)}, u32[]{:S(2)}) collective-permute-start(bf16[2,64,512]{2,1,0:T(8,128)(2,1)} %get-tuple-element.69), channel_id=1, source_target_pairs={{0,2},{1,3},{2,4},{3,5},{4,6},{5,7},{6,8},{7,9},{8,10},{9,11},{10,... | collective-permute-start | bytes 393224 | tf_op jit(solution)/shard_map/ppermute | solution.py:46
  67.0 1.3 collective-permute-start.3
  68.4 7.5 %collective-permute-done.15.refs_14_ = bf16[2,64,512]{2,1,0:T(8,128)(2,1)S(1)} collective-permute-done((bf16[2,64,512]{2,1,0:T(8,128)(2,1)S(1)}, bf16[2,64,512]{2,1,0:T(8,128)(2,1)S(1)}, u32[]{:S(2)}, u32[]{:S(2)}) %collective-permute-start.15) | collective-permute-done | bytes 131104 | tf_op jit(solution)/shard_map/ppermute | solution.py:46
  77.3 1.3 collective-permute-start.5
  78.6 5.1 %collective-permute-start.6 = (bf16[2,64,512]{2,1,0:T(8,128)(2,1)}, bf16[2,64,512]{2,1,0:T(8,128)(2,1)S(1)}, u32[]{:S(2)}, u32[]{:S(2)}) collective-permute-start(bf16[2,64,512]{2,1,0:T(8,128)(2,1)} %get-tuple-element.73), channel_id=1, source_target_pairs={{0,8},{1,9},{2,10},{3,11},{4,12},{5,13},{6,14},{7,15},{16,24},{17,... | collective-permute-start | bytes 393224 | tf_op jit(solution)/shard_map/ppermute | solution.py:46
  84.2 1.3 collective-permute-start.8
  85.6 1.3 collective-permute-start.9
  86.9 3.8 %collective-permute-start = (bf16[2,192,512]{2,1,0:T(8,128)(2,1)}, bf16[2,192,512]{2,1,0:T(8,128)(2,1)S(1)}, u32[]{:S(2)}, u32[]{:S(2)}) collective-permute-start(bf16[2,192,512]{2,1,0:T(8,128)(2,1)} %get-tuple-element.67), channel_id=1, source_target_pairs={{0,1},{1,2},{2,3},{3,4},{4,5},{5,6},{6,7},{7,8},{8,9},{9,10},{10,1... | collective-permute-start | bytes 1179656 | tf_op jit(solution)/shard_map/ppermute | solution.py:46
  90.8 1.3 collective-permute-start.1
  96.4 28.0 %attend.3 = (bf16[384,1536]{1,0:T(8,128)(2,1)}, bf16[384,1536]{1,0:T(8,128)(2,1)}, f32[2,384,512]{2,1,0:T(8,128)}, bf16[2,192,512]{2,1,0:T(8,128)(2,1)}, bf16[2,...) custom-call(s32[1,384]{1,0:T(1,128)} %shift-right-logical_xor_fusion, ...), custom_call_target="tpu_custom_call" | custom-call | flops 2717908992 | bytes 9437184 | tf_op jit(solution)/shard_map/attend/pallas_call | solution.py:242
  124.5 1.3 collective-permute-start.42
  125.8 6.5 %collective-permute-start.43 = (bf16[2,64,512]{2,1,0:T(8,128)(2,1)}, bf16[2,64,512]{2,1,0:T(8,128)(2,1)S(1)}, u32[]{:S(2)}, u32[]{:S(2)}) collective-permute-start(bf16[2,64,512]{2,1,0:T(8,128)(2,1)} %get-tuple-element.119), channel_id=1, source_target_pairs={{0,2},{1,3},{2,4},{3,5},{4,6},{5,7},{6,8},{7,9},{8,10},{9,11},{10,... | collective-permute-start | bytes 393224 | tf_op jit(solution)/shard_map/ppermute | solution.py:46
  132.3 1.3 collective-permute-start.44
  133.7 7.8 %collective-permute-start.45 = (bf16[2,64,512]{2,1,0:T(8,128)(2,1)}, bf16[2,64,512]{2,1,0:T(8,128)(2,1)S(1)}, u32[]{:S(2)}, u32[]{:S(2)}) collective-permute-start(bf16[2,64,512]{2,1,0:T(8,128)(2,1)} %get-tuple-element.121), channel_id=1, source_target_pairs={{0,4},{1,5},{2,6},{3,7},{4,8},{5,9},{6,10},{7,11},{8,12},{9,13},{1... | collective-permute-start | bytes 393224 | tf_op jit(solution)/shard_map/ppermute | solution.py:46
  141.5 1.3 collective-permute-start.46
  142.8 5.5 %collective-permute-start.47 = (bf16[2,64,512]{2,1,0:T(8,128)(2,1)}, bf16[2,64,512]{2,1,0:T(8,128)(2,1)S(1)}, u32[]{:S(2)}, u32[]{:S(2)}) collective-permute-start(bf16[2,64,512]{2,1,0:T(8,128)(2,1)} %get-tuple-element.123), channel_id=1, source_target_pairs={{0,8},{1,9},{2,10},{3,11},{4,12},{5,13},{6,14},{7,15},{16,24},{17,... | collective-permute-start | bytes 393224 | tf_op jit(solution)/shard_map/ppermute | solution.py:46
  148.3 28.2 %attend.4 = (bf16[384,1536]{1,0:T(8,128)(2,1)}, bf16[384,1536]{1,0:T(8,128)(2,1)}, f32[2,384,512]{2,1,0:T(8,128)}, bf16[2,192,512]{2,1,0:T(8,128)(2,1)}, bf16[2,...) custom-call(s32[1,384]{1,0:T(1,128)} %shift-right-logical_xor_fusion, ...), custom_call_target="tpu_custom_call", output_to_operand_aliasing={{0}: (15, {}), {1}: (16, {})} | custom-call | flops 2717908992 | bytes 9437184 | tf_op jit(solution)/shard_map/attend/pallas_call | solution.py:242
  176.5 1.3 collective-permute-start.40
  179.2 4.6 %collective-permute-start.35 = (bf16[2,64,512]{2,1,0:T(8,128)(2,1)}, bf16[2,64,512]{2,1,0:T(8,128)(2,1)S(1)}, u32[]{:S(2)}, u32[]{:S(2)}) collective-permute-start(bf16[2,64,512]{2,1,0:T(8,128)(2,1)} %get-tuple-element.110), channel_id=1, source_target_pairs={{0,2},{1,3},{2,4},{3,5},{4,6},{5,7},{6,8},{7,9},{8,10},{9,11},{10,... | collective-permute-start | bytes 393224 | tf_op jit(solution)/shard_map/ppermute | solution.py:46
  185.2 5.1 %collective-permute-start.37 = (bf16[2,64,512]{2,1,0:T(8,128)(2,1)}, bf16[2,64,512]{2,1,0:T(8,128)(2,1)S(1)}, u32[]{:S(2)}, u32[]{:S(2)}) collective-permute-start(bf16[2,64,512]{2,1,0:T(8,128)(2,1)} %get-tuple-element.112), channel_id=1, source_target_pairs={{0,4},{1,5},{2,6},{3,7},{4,8},{5,9},{6,10},{7,11},{8,12},{9,13},{1... | collective-permute-start | bytes 393224 | tf_op jit(solution)/shard_map/ppermute | solution.py:46
  190.3 28.2 %attend.5 = (bf16[384,1536]{1,0:T(8,128)(2,1)}, bf16[384,1536]{1,0:T(8,128)(2,1)}, f32[2,384,512]{2,1,0:T(8,128)}, bf16[2,192,512]{2,1,0:T(8,128)(2,1)}, bf16[2,...) custom-call(s32[1,384]{1,0:T(1,128)} %shift-right-logical_xor_fusion, ...), custom_call_target="tpu_custom_call", output_to_operand_aliasing={{0}: (15, {}), {1}: (16, {})} | custom-call | flops 2717908992 | bytes 9437184 | tf_op jit(solution)/shard_map/attend/pallas_call | solution.py:242
  219.9 5.5 %collective-permute-start.39 = (bf16[2,64,512]{2,1,0:T(8,128)(2,1)S(1)}, bf16[2,64,512]{2,1,0:T(8,128)(2,1)S(1)}, u32[]{:S(2)}, u32[]{:S(2)}) collective-permute-start(bf16[2,64,512]{2,1,0:T(8,128)(2,1)S(1)} %copy-done.47), channel_id=1, source_target_pairs={{0,8},{1,9},{2,10},{3,11},{4,12},{5,13},{6,14},{7,15},{16,24},{17,... | collective-permute-start | bytes 393224 | tf_op jit(solution)/shard_map/ppermute | solution.py:46
  226.7 5.0 %collective-permute-start.27 = (bf16[2,64,512]{2,1,0:T(8,128)(2,1)}, bf16[2,64,512]{2,1,0:T(8,128)(2,1)S(1)}, u32[]{:S(2)}, u32[]{:S(2)}) collective-permute-start(bf16[2,64,512]{2,1,0:T(8,128)(2,1)} %get-tuple-element.101), channel_id=1, source_target_pairs={{0,2},{1,3},{2,4},{3,5},{4,6},{5,7},{6,8},{7,9},{8,10},{9,11},{10,... | collective-permute-start | bytes 393224 | tf_op jit(solution)/shard_map/ppermute | solution.py:46
  231.7 1.3 collective-permute-start.41
  234.3 1.3 collective-permute-start.28
  235.7 6.1 %collective-permute-start.33 = (bf16[2,192,512]{2,1,0:T(8,128)(2,1)}, bf16[2,192,512]{2,1,0:T(8,128)(2,1)S(1)}, u32[]{:S(2)}, u32[]{:S(2)}) collective-permute-start(bf16[2,192,512]{2,1,0:T(8,128)(2,1)} %get-tuple-element.108), channel_id=1, source_target_pairs={{0,1},{1,2},{2,3},{3,4},{4,5},{5,6},{6,7},{7,8},{8,9},{9,10},{10,1... | collective-permute-start | bytes 1179656 | tf_op jit(solution)/shard_map/ppermute | solution.py:46
  241.8 7.1 %collective-permute-done.28.refs_4_ = bf16[2,64,512]{2,1,0:T(8,128)(2,1)S(1)} collective-permute-done((bf16[2,64,512]{2,1,0:T(8,128)(2,1)}, bf16[2,64,512]{2,1,0:T(8,128)(2,1)S(1)}, u32[]{:S(2)}, u32[]{:S(2)}) %collective-permute-start.28) | collective-permute-done | bytes 131104 | tf_op jit(solution)/shard_map/ppermute | solution.py:46
  250.3 3.1 %collective-permute-start.25 = (bf16[2,192,512]{2,1,0:T(8,128)(2,1)}, bf16[2,192,512]{2,1,0:T(8,128)(2,1)S(1)}, u32[]{:S(2)}, u32[]{:S(2)}) collective-permute-start(bf16[2,192,512]{2,1,0:T(8,128)(2,1)} %get-tuple-element.99), channel_id=1, source_target_pairs={{0,1},{1,2},{2,3},{3,4},{4,5},{5,6},{6,7},{7,8},{8,9},{9,10},{10,1... | collective-permute-start | bytes 1179656 | tf_op jit(solution)/shard_map/ppermute | solution.py:46
  253.4 4.0 %collective-permute-start.29 = (bf16[2,64,512]{2,1,0:T(8,128)(2,1)}, bf16[2,64,512]{2,1,0:T(8,128)(2,1)}, u32[]{:S(2)}, u32[]{:S(2)}) collective-permute-start(bf16[2,64,512]{2,1,0:T(8,128)(2,1)} %get-tuple-element.103), channel_id=1, source_target_pairs={{0,4},{1,5},{2,6},{3,7},{4,8},{5,9},{6,10},{7,11},{8,12},{9,13},{1... | collective-permute-start | bytes 393224 | tf_op jit(solution)/shard_map/ppermute | solution.py:46
  258.7 6.7 %collective-permute-start.31 = (bf16[2,64,512]{2,1,0:T(8,128)(2,1)}, bf16[2,64,512]{2,1,0:T(8,128)(2,1)}, u32[]{:S(2)}, u32[]{:S(2)}) collective-permute-start(bf16[2,64,512]{2,1,0:T(8,128)(2,1)} %get-tuple-element.105), channel_id=1, source_target_pairs={{0,8},{1,9},{2,10},{3,11},{4,12},{5,13},{6,14},{7,15},{16,24},{17,... | collective-permute-start | bytes 393224 | tf_op jit(solution)/shard_map/ppermute | solution.py:46
  265.4 3.9 %finish.3 = (bf16[384,1536]{1,0:T(8,128)(2,1)}, bf16[384,1536]{1,0:T(8,128)(2,1)}) custom-call(s32[12]{0:T(128)} %concatenate.3.ids_ref, f32[2,384,512]{2,1,0:T(8,128)} %get-tuple-element.115.own_ref, bf16[2,192,512]{2,1,0:T(8,128)(2,1)} %copy-done.4, bf16[2,192,512]{2,1,0:T(8,128)(2,1)} %copy-done.5, bf16[2,64,512]{2,1,0:T(8,128)(2,1)} %collective-permute-done.42.refs_2_, ...), custom_call_target="tpu_custom_call" | custom-call | bytes 5898240 | tf_op jit(solution)/shard_map/finish/pallas_call | solution.py:280
  269.4 3.9 %finish.4 = (bf16[384,1536]{1,0:T(8,128)(2,1)}, bf16[384,1536]{1,0:T(8,128)(2,1)}) custom-call(s32[12]{0:T(128)} %concatenate.3.ids_ref, f32[2,384,512]{2,1,0:T(8,128)} %get-tuple-element.106.own_ref, bf16[2,192,512]{2,1,0:T(8,128)(2,1)} %copy-done.2, bf16[2,192,512]{2,1,0:T(8,128)(2,1)} %copy-done.3, ...), custom_call_target="tpu_custom_call", output_to_operand_aliasing={{0}: (10, {}), {1}: (11, {})} | custom-call | bytes 5898240 | tf_op jit(solution)/shard_map/finish/pallas_call | solution.py:280
  274.3 3.9 %finish.5 = (bf16[384,1536]{1,0:T(8,128)(2,1)}, bf16[384,1536]{1,0:T(8,128)(2,1)}) custom-call(s32[12]{0:T(128)} %concatenate.3.ids_ref, f32[2,384,512]{2,1,0:T(8,128)} %get-tuple-element.97.own_ref, bf16[2,192,512]{2,1,0:T(8,128)(2,1)} %copy-done, bf16[2,192,512]{2,1,0:T(8,128)(2,1)} %copy-done.1, ...), custom_call_target="tpu_custom_call", output_to_operand_aliasing={{0}: (10, {}), {1}: (11, {})} | custom-call | bytes 5898240 | tf_op jit(solution)/shard_map/finish/pallas_call | solution.py:280
  (190 shorter events, 26.3 us)
Async XLA Ops:
  12.1 18.5 %collective-permute-start.18 = (bf16[2,64,512]{2,1,0:T(8,128)(2,1)}, bf16[2,64,512]{2,1,0:T(8,128)(2,1)}, u32[]{:S(2)}, u32[]{:S(2)}) collective-permute-start(bf16[2,64,512]{2,1,0:T(8,128)(2,1)} %get-tuple-element.85), channel_id=1, source_target_pairs={{0,2},{1,3},{2,4},{3,5},{4,6},{5,7},{6,8},{7,9},{8,10},{9,11},{10,... | collective-permute-start | bytes 393224 | tf_op jit(solution)/shard_map/ppermute | solution.py:46
  17.6 20.6 %collective-permute-start.19 = (bf16[2,64,512]{2,1,0:T(8,128)(2,1)}, bf16[2,64,512]{2,1,0:T(8,128)(2,1)S(1)}, u32[]{:S(2)}, u32[]{:S(2)}) collective-permute-start(bf16[2,64,512]{2,1,0:T(8,128)(2,1)} %get-tuple-element.86), channel_id=1, source_target_pairs={{2,0},{3,1},{4,2},{5,3},{6,4},{7,5},{8,6},{9,7},{10,8},{11,9},{12,... | collective-permute-start | bytes 393224 | tf_op jit(solution)/shard_map/ppermute | solution.py:46
  18.9 21.9 %collective-permute-start.20 = (bf16[2,64,512]{2,1,0:T(8,128)(2,1)}, bf16[2,64,512]{2,1,0:T(8,128)(2,1)S(1)}, u32[]{:S(2)}, u32[]{:S(2)}) collective-permute-start(bf16[2,64,512]{2,1,0:T(8,128)(2,1)} %get-tuple-element.87), channel_id=1, source_target_pairs={{0,4},{1,5},{2,6},{3,7},{4,8},{5,9},{6,10},{7,11},{8,12},{9,13},{1... | collective-permute-start | bytes 393224 | tf_op jit(solution)/shard_map/ppermute | solution.py:46
  23.8 19.1 %collective-permute-start.21 = (bf16[2,64,512]{2,1,0:T(8,128)(2,1)}, bf16[2,64,512]{2,1,0:T(8,128)(2,1)S(1)}, u32[]{:S(2)}, u32[]{:S(2)}) collective-permute-start(bf16[2,64,512]{2,1,0:T(8,128)(2,1)} %get-tuple-element.88), channel_id=1, source_target_pairs={{4,0},{5,1},{6,2},{7,3},{8,4},{9,5},{10,6},{11,7},{12,8},{13,9},{1... | collective-permute-start | bytes 393224 | tf_op jit(solution)/shard_map/ppermute | solution.py:46
  25.1 24.9 %collective-permute-start.22 = (bf16[2,64,512]{2,1,0:T(8,128)(2,1)}, bf16[2,64,512]{2,1,0:T(8,128)(2,1)S(1)}, u32[]{:S(2)}, u32[]{:S(2)}) collective-permute-start(bf16[2,64,512]{2,1,0:T(8,128)(2,1)} %get-tuple-element.89), channel_id=1, source_target_pairs={{0,8},{1,9},{2,10},{3,11},{4,12},{5,13},{6,14},{7,15},{16,24},{17,... | collective-permute-start | bytes 393224 | tf_op jit(solution)/shard_map/ppermute | solution.py:46
  30.6 20.7 %collective-permute-start.23 = (bf16[2,64,512]{2,1,0:T(8,128)(2,1)}, bf16[2,64,512]{2,1,0:T(8,128)(2,1)S(1)}, u32[]{:S(2)}, u32[]{:S(2)}) collective-permute-start(bf16[2,64,512]{2,1,0:T(8,128)(2,1)} %get-tuple-element.90), channel_id=1, source_target_pairs={{8,0},{9,1},{10,2},{11,3},{12,4},{13,5},{14,6},{15,7},{24,16},{25,... | collective-permute-start | bytes 393224 | tf_op jit(solution)/shard_map/ppermute | solution.py:46
  38.3 19.5 %collective-permute-start.10 = (bf16[2,64,512]{2,1,0:T(8,128)(2,1)S(1)}, bf16[2,64,512]{2,1,0:T(8,128)(2,1)S(1)}, u32[]{:S(2)}, u32[]{:S(2)}) collective-permute-start(bf16[2,64,512]{2,1,0:T(8,128)(2,1)S(1)} %copy-done.54), channel_id=1, source_target_pairs={{0,2},{1,3},{2,4},{3,5},{4,6},{5,7},{6,8},{7,9},{8,10},{9,11},{10,... | collective-permute-start | bytes 393224 | tf_op jit(solution)/shard_map/ppermute | solution.py:46
  41.5 17.6 %collective-permute-start.11 = (bf16[2,64,512]{2,1,0:T(8,128)(2,1)S(1)}, bf16[2,64,512]{2,1,0:T(8,128)(2,1)S(1)}, u32[]{:S(2)}, u32[]{:S(2)}) collective-permute-start(bf16[2,64,512]{2,1,0:T(8,128)(2,1)S(1)} %copy-done.53), channel_id=1, source_target_pairs={{2,0},{3,1},{4,2},{5,3},{6,4},{7,5},{8,6},{9,7},{10,8},{11,9},{12,... | collective-permute-start | bytes 393224 | tf_op jit(solution)/shard_map/ppermute | solution.py:46
  43.5 17.0 %collective-permute-start.12 = (bf16[2,64,512]{2,1,0:T(8,128)(2,1)S(1)}, bf16[2,64,512]{2,1,0:T(8,128)(2,1)S(1)}, u32[]{:S(2)}, u32[]{:S(2)}) collective-permute-start(bf16[2,64,512]{2,1,0:T(8,128)(2,1)S(1)} %copy-done.52), channel_id=1, source_target_pairs={{0,4},{1,5},{2,6},{3,7},{4,8},{5,9},{6,10},{7,11},{8,12},{9,13},{1... | collective-permute-start | bytes 393224 | tf_op jit(solution)/shard_map/ppermute | solution.py:46
  50.0 11.8 %collective-permute-start.13 = (bf16[2,64,512]{2,1,0:T(8,128)(2,1)S(1)}, bf16[2,64,512]{2,1,0:T(8,128)(2,1)S(1)}, u32[]{:S(2)}, u32[]{:S(2)}) collective-permute-start(bf16[2,64,512]{2,1,0:T(8,128)(2,1)S(1)} %copy-done.51), channel_id=1, source_target_pairs={{4,0},{5,1},{6,2},{7,3},{8,4},{9,5},{10,6},{11,7},{12,8},{13,9},{1... | collective-permute-start | bytes 393224 | tf_op jit(solution)/shard_map/ppermute | solution.py:46
  51.3 15.6 %collective-permute-start.14 = (bf16[2,64,512]{2,1,0:T(8,128)(2,1)S(1)}, bf16[2,64,512]{2,1,0:T(8,128)(2,1)S(1)}, u32[]{:S(2)}, u32[]{:S(2)}) collective-permute-start(bf16[2,64,512]{2,1,0:T(8,128)(2,1)S(1)} %copy-done.50), channel_id=1, source_target_pairs={{0,8},{1,9},{2,10},{3,11},{4,12},{5,13},{6,14},{7,15},{16,24},{17,... | collective-permute-start | bytes 393224 | tf_op jit(solution)/shard_map/ppermute | solution.py:46
  57.8 33.0 %collective-permute-start.16 = (bf16[2,192,512]{2,1,0:T(8,128)(2,1)S(1)}, bf16[2,192,512]{2,1,0:T(8,128)(2,1)S(1)}, u32[]{:S(2)}, u32[]{:S(2)}) collective-permute-start(bf16[2,192,512]{2,1,0:T(8,128)(2,1)S(1)} %copy-done.24), channel_id=1, source_target_pairs={{0,1},{1,2},{2,3},{3,4},{4,5},{5,6},{6,7},{7,8},{8,9},{9,10},{10,1... | collective-permute-start | bytes 1179656 | tf_op jit(solution)/shard_map/ppermute | solution.py:46
  59.2 33.9 %collective-permute-start.17 = (bf16[2,192,512]{2,1,0:T(8,128)(2,1)S(1)}, bf16[2,192,512]{2,1,0:T(8,128)(2,1)S(1)}, u32[]{:S(2)}, u32[]{:S(2)}) collective-permute-start(bf16[2,192,512]{2,1,0:T(8,128)(2,1)S(1)} %copy-done.23), channel_id=1, source_target_pairs={{1,0},{2,1},{3,2},{4,3},{5,4},{6,5},{7,6},{8,7},{9,8},{10,9},{11,1... | collective-permute-start | bytes 1179656 | tf_op jit(solution)/shard_map/ppermute | solution.py:46
  60.5 15.5 %collective-permute-start.15 = (bf16[2,64,512]{2,1,0:T(8,128)(2,1)S(1)}, bf16[2,64,512]{2,1,0:T(8,128)(2,1)S(1)}, u32[]{:S(2)}, u32[]{:S(2)}) collective-permute-start(bf16[2,64,512]{2,1,0:T(8,128)(2,1)S(1)} %copy-done.49), channel_id=1, source_target_pairs={{8,0},{9,1},{10,2},{11,3},{12,4},{13,5},{14,6},{15,7},{24,16},{25,... | collective-permute-start | bytes 393224 | tf_op jit(solution)/shard_map/ppermute | solution.py:46
  61.8 15.4 %collective-permute-start.2 = (bf16[2,64,512]{2,1,0:T(8,128)(2,1)}, bf16[2,64,512]{2,1,0:T(8,128)(2,1)S(1)}, u32[]{:S(2)}, u32[]{:S(2)}) collective-permute-start(bf16[2,64,512]{2,1,0:T(8,128)(2,1)} %get-tuple-element.69), channel_id=1, source_target_pairs={{0,2},{1,3},{2,4},{3,5},{4,6},{5,7},{6,8},{7,9},{8,10},{9,11},{10,... | collective-permute-start | bytes 393224 | tf_op jit(solution)/shard_map/ppermute | solution.py:46
  67.0 11.6 %collective-permute-start.3 = (bf16[2,64,512]{2,1,0:T(8,128)(2,1)}, bf16[2,64,512]{2,1,0:T(8,128)(2,1)S(1)}, u32[]{:S(2)}, u32[]{:S(2)}) collective-permute-start(bf16[2,64,512]{2,1,0:T(8,128)(2,1)} %get-tuple-element.70), channel_id=1, source_target_pairs={{2,0},{3,1},{4,2},{5,3},{6,4},{7,5},{8,6},{9,7},{10,8},{11,9},{12,... | collective-permute-start | bytes 393224 | tf_op jit(solution)/shard_map/ppermute | solution.py:46
  76.0 8.2 %collective-permute-start.4 = (bf16[2,64,512]{2,1,0:T(8,128)(2,1)}, bf16[2,64,512]{2,1,0:T(8,128)(2,1)S(1)}, u32[]{:S(2)}, u32[]{:S(2)}) collective-permute-start(bf16[2,64,512]{2,1,0:T(8,128)(2,1)} %get-tuple-element.71), channel_id=1, source_target_pairs={{0,4},{1,5},{2,6},{3,7},{4,8},{5,9},{6,10},{7,11},{8,12},{9,13},{1... | collective-permute-start | bytes 393224 | tf_op jit(solution)/shard_map/ppermute | solution.py:46
  77.3 8.3 %collective-permute-start.5 = (bf16[2,64,512]{2,1,0:T(8,128)(2,1)}, bf16[2,64,512]{2,1,0:T(8,128)(2,1)S(1)}, u32[]{:S(2)}, u32[]{:S(2)}) collective-permute-start(bf16[2,64,512]{2,1,0:T(8,128)(2,1)} %get-tuple-element.72), channel_id=1, source_target_pairs={{4,0},{5,1},{6,2},{7,3},{8,4},{9,5},{10,6},{11,7},{12,8},{13,9},{1... | collective-permute-start | bytes 393224 | tf_op jit(solution)/shard_map/ppermute | solution.py:46
  78.6 8.3 %collective-permute-start.6 = (bf16[2,64,512]{2,1,0:T(8,128)(2,1)}, bf16[2,64,512]{2,1,0:T(8,128)(2,1)S(1)}, u32[]{:S(2)}, u32[]{:S(2)}) collective-permute-start(bf16[2,64,512]{2,1,0:T(8,128)(2,1)} %get-tuple-element.73), channel_id=1, source_target_pairs={{0,8},{1,9},{2,10},{3,11},{4,12},{5,13},{6,14},{7,15},{16,24},{17,... | collective-permute-start | bytes 393224 | tf_op jit(solution)/shard_map/ppermute | solution.py:46
  84.2 41.6 %collective-permute-start.8 = (bf16[2,192,512]{2,1,0:T(8,128)(2,1)S(1)}, bf16[2,192,512]{2,1,0:T(8,128)(2,1)S(1)}, u32[]{:S(2)}, u32[]{:S(2)}) collective-permute-start(bf16[2,192,512]{2,1,0:T(8,128)(2,1)S(1)} %copy-done.21), channel_id=1, source_target_pairs={{0,1},{1,2},{2,3},{3,4},{4,5},{5,6},{6,7},{7,8},{8,9},{9,10},{10,1... | collective-permute-start | bytes 1179656 | tf_op jit(solution)/shard_map/ppermute | solution.py:46
  85.6 46.7 %collective-permute-start.9 = (bf16[2,192,512]{2,1,0:T(8,128)(2,1)S(1)}, bf16[2,192,512]{2,1,0:T(8,128)(2,1)}, u32[]{:S(2)}, u32[]{:S(2)}) collective-permute-start(bf16[2,192,512]{2,1,0:T(8,128)(2,1)S(1)} %copy-done.20), channel_id=1, source_target_pairs={{1,0},{2,1},{3,2},{4,3},{5,4},{6,5},{7,6},{8,7},{9,8},{10,9},{11,1... | collective-permute-start | bytes 1179656 | tf_op jit(solution)/shard_map/ppermute | solution.py:46
  86.9 46.7 %collective-permute-start = (bf16[2,192,512]{2,1,0:T(8,128)(2,1)}, bf16[2,192,512]{2,1,0:T(8,128)(2,1)S(1)}, u32[]{:S(2)}, u32[]{:S(2)}) collective-permute-start(bf16[2,192,512]{2,1,0:T(8,128)(2,1)} %get-tuple-element.67), channel_id=1, source_target_pairs={{0,1},{1,2},{2,3},{3,4},{4,5},{5,6},{6,7},{7,8},{8,9},{9,10},{10,1... | collective-permute-start | bytes 1179656 | tf_op jit(solution)/shard_map/ppermute | solution.py:46
  90.8 50.7 %collective-permute-start.1 = (bf16[2,192,512]{2,1,0:T(8,128)(2,1)}, bf16[2,192,512]{2,1,0:T(8,128)(2,1)S(1)}, u32[]{:S(2)}, u32[]{:S(2)}) collective-permute-start(bf16[2,192,512]{2,1,0:T(8,128)(2,1)} %get-tuple-element.68), channel_id=1, source_target_pairs={{1,0},{2,1},{3,2},{4,3},{5,4},{6,5},{7,6},{8,7},{9,8},{10,9},{11,1... | collective-permute-start | bytes 1179656 | tf_op jit(solution)/shard_map/ppermute | solution.py:46
  93.1 31.4 %collective-permute-start.7 = (bf16[2,64,512]{2,1,0:T(8,128)(2,1)}, bf16[2,64,512]{2,1,0:T(8,128)(2,1)S(1)}, u32[]{:S(2)}, u32[]{:S(2)}) collective-permute-start(bf16[2,64,512]{2,1,0:T(8,128)(2,1)} %get-tuple-element.74), channel_id=1, source_target_pairs={{8,0},{9,1},{10,2},{11,3},{12,4},{13,5},{14,6},{15,7},{24,16},{25,... | collective-permute-start | bytes 393224 | tf_op jit(solution)/shard_map/ppermute | solution.py:46
  124.5 18.3 %collective-permute-start.42 = (bf16[2,64,512]{2,1,0:T(8,128)(2,1)}, bf16[2,64,512]{2,1,0:T(8,128)(2,1)}, u32[]{:S(2)}, u32[]{:S(2)}) collective-permute-start(bf16[2,64,512]{2,1,0:T(8,128)(2,1)} %get-tuple-element.118), channel_id=1, source_target_pairs={{2,0},{3,1},{4,2},{5,3},{6,4},{7,5},{8,6},{9,7},{10,8},{11,9},{12,... | collective-permute-start | bytes 393224 | tf_op jit(solution)/shard_map/ppermute | solution.py:46
  125.8 50.7 %collective-permute-start.43 = (bf16[2,64,512]{2,1,0:T(8,128)(2,1)}, bf16[2,64,512]{2,1,0:T(8,128)(2,1)S(1)}, u32[]{:S(2)}, u32[]{:S(2)}) collective-permute-start(bf16[2,64,512]{2,1,0:T(8,128)(2,1)} %get-tuple-element.119), channel_id=1, source_target_pairs={{0,2},{1,3},{2,4},{3,5},{4,6},{5,7},{6,8},{7,9},{8,10},{9,11},{10,... | collective-permute-start | bytes 393224 | tf_op jit(solution)/shard_map/ppermute | solution.py:46
  132.3 45.5 %collective-permute-start.44 = (bf16[2,64,512]{2,1,0:T(8,128)(2,1)}, bf16[2,64,512]{2,1,0:T(8,128)(2,1)S(1)}, u32[]{:S(2)}, u32[]{:S(2)}) collective-permute-start(bf16[2,64,512]{2,1,0:T(8,128)(2,1)} %get-tuple-element.120), channel_id=1, source_target_pairs={{4,0},{5,1},{6,2},{7,3},{8,4},{9,5},{10,6},{11,7},{12,8},{13,9},{1... | collective-permute-start | bytes 393224 | tf_op jit(solution)/shard_map/ppermute | solution.py:46
  133.7 45.5 %collective-permute-start.45 = (bf16[2,64,512]{2,1,0:T(8,128)(2,1)}, bf16[2,64,512]{2,1,0:T(8,128)(2,1)S(1)}, u32[]{:S(2)}, u32[]{:S(2)}) collective-permute-start(bf16[2,64,512]{2,1,0:T(8,128)(2,1)} %get-tuple-element.121), channel_id=1, source_target_pairs={{0,4},{1,5},{2,6},{3,7},{4,8},{5,9},{6,10},{7,11},{8,12},{9,13},{1... | collective-permute-start | bytes 393224 | tf_op jit(solution)/shard_map/ppermute | solution.py:46
  141.5 42.3 %collective-permute-start.46 = (bf16[2,64,512]{2,1,0:T(8,128)(2,1)}, bf16[2,64,512]{2,1,0:T(8,128)(2,1)S(1)}, u32[]{:S(2)}, u32[]{:S(2)}) collective-permute-start(bf16[2,64,512]{2,1,0:T(8,128)(2,1)} %get-tuple-element.122), channel_id=1, source_target_pairs={{8,0},{9,1},{10,2},{11,3},{12,4},{13,5},{14,6},{15,7},{24,16},{25,... | collective-permute-start | bytes 393224 | tf_op jit(solution)/shard_map/ppermute | solution.py:46
  142.8 42.3 %collective-permute-start.47 = (bf16[2,64,512]{2,1,0:T(8,128)(2,1)}, bf16[2,64,512]{2,1,0:T(8,128)(2,1)S(1)}, u32[]{:S(2)}, u32[]{:S(2)}) collective-permute-start(bf16[2,64,512]{2,1,0:T(8,128)(2,1)} %get-tuple-element.123), channel_id=1, source_target_pairs={{0,8},{1,9},{2,10},{3,11},{4,12},{5,13},{6,14},{7,15},{16,24},{17,... | collective-permute-start | bytes 393224 | tf_op jit(solution)/shard_map/ppermute | solution.py:46
  176.5 73.7 %collective-permute-start.40 = (bf16[2,192,512]{2,1,0:T(8,128)(2,1)S(1)}, bf16[2,192,512]{2,1,0:T(8,128)(2,1)S(1)}, u32[]{:S(2)}, u32[]{:S(2)}) collective-permute-start(bf16[2,192,512]{2,1,0:T(8,128)(2,1)S(1)} %copy-done.22), channel_id=1, source_target_pairs={{1,0},{2,1},{3,2},{4,3},{5,4},{6,5},{7,6},{8,7},{9,8},{10,9},{11,1... | collective-permute-start | bytes 1179656 | tf_op jit(solution)/shard_map/ppermute | solution.py:46
  177.9 40.7 %collective-permute-start.34 = (bf16[2,64,512]{2,1,0:T(8,128)(2,1)}, bf16[2,64,512]{2,1,0:T(8,128)(2,1)S(1)}, u32[]{:S(2)}, u32[]{:S(2)}) collective-permute-start(bf16[2,64,512]{2,1,0:T(8,128)(2,1)} %get-tuple-element.109), channel_id=1, source_target_pairs={{2,0},{3,1},{4,2},{5,3},{6,4},{7,5},{8,6},{9,7},{10,8},{11,9},{12,... | collective-permute-start | bytes 393224 | tf_op jit(solution)/shard_map/ppermute | solution.py:46
  179.2 40.7 %collective-permute-start.35 = (bf16[2,64,512]{2,1,0:T(8,128)(2,1)}, bf16[2,64,512]{2,1,0:T(8,128)(2,1)S(1)}, u32[]{:S(2)}, u32[]{:S(2)}) collective-permute-start(bf16[2,64,512]{2,1,0:T(8,128)(2,1)} %get-tuple-element.110), channel_id=1, source_target_pairs={{0,2},{1,3},{2,4},{3,5},{4,6},{5,7},{6,8},{7,9},{8,10},{9,11},{10,... | collective-permute-start | bytes 393224 | tf_op jit(solution)/shard_map/ppermute | solution.py:46
  183.8 41.5 %collective-permute-start.36 = (bf16[2,64,512]{2,1,0:T(8,128)(2,1)}, bf16[2,64,512]{2,1,0:T(8,128)(2,1)S(1)}, u32[]{:S(2)}, u32[]{:S(2)}) collective-permute-start(bf16[2,64,512]{2,1,0:T(8,128)(2,1)} %get-tuple-element.111), channel_id=1, source_target_pairs={{4,0},{5,1},{6,2},{7,3},{8,4},{9,5},{10,6},{11,7},{12,8},{13,9},{1... | collective-permute-start | bytes 393224 | tf_op jit(solution)/shard_map/ppermute | solution.py:46
  185.2 41.5 %collective-permute-start.37 = (bf16[2,64,512]{2,1,0:T(8,128)(2,1)}, bf16[2,64,512]{2,1,0:T(8,128)(2,1)S(1)}, u32[]{:S(2)}, u32[]{:S(2)}) collective-permute-start(bf16[2,64,512]{2,1,0:T(8,128)(2,1)} %get-tuple-element.112), channel_id=1, source_target_pairs={{0,4},{1,5},{2,6},{3,7},{4,8},{5,9},{6,10},{7,11},{8,12},{9,13},{1... | collective-permute-start | bytes 393224 | tf_op jit(solution)/shard_map/ppermute | solution.py:46
  218.5 13.1 %collective-permute-start.38 = (bf16[2,64,512]{2,1,0:T(8,128)(2,1)S(1)}, bf16[2,64,512]{2,1,0:T(8,128)(2,1)S(1)}, u32[]{:S(2)}, u32[]{:S(2)}) collective-permute-start(bf16[2,64,512]{2,1,0:T(8,128)(2,1)S(1)} %copy-done.48), channel_id=1, source_target_pairs={{8,0},{9,1},{10,2},{11,3},{12,4},{13,5},{14,6},{15,7},{24,16},{25,... | collective-permute-start | bytes 393224 | tf_op jit(solution)/shard_map/ppermute | solution.py:46
  219.9 13.1 %collective-permute-start.39 = (bf16[2,64,512]{2,1,0:T(8,128)(2,1)S(1)}, bf16[2,64,512]{2,1,0:T(8,128)(2,1)S(1)}, u32[]{:S(2)}, u32[]{:S(2)}) collective-permute-start(bf16[2,64,512]{2,1,0:T(8,128)(2,1)S(1)} %copy-done.47), channel_id=1, source_target_pairs={{0,8},{1,9},{2,10},{3,11},{4,12},{5,13},{6,14},{7,15},{16,24},{17,... | collective-permute-start | bytes 393224 | tf_op jit(solution)/shard_map/ppermute | solution.py:46
  225.3 9.0 %collective-permute-start.26 = (bf16[2,64,512]{2,1,0:T(8,128)(2,1)}, bf16[2,64,512]{2,1,0:T(8,128)(2,1)S(1)}, u32[]{:S(2)}, u32[]{:S(2)}) collective-permute-start(bf16[2,64,512]{2,1,0:T(8,128)(2,1)} %get-tuple-element.100), channel_id=1, source_target_pairs={{2,0},{3,1},{4,2},{5,3},{6,4},{7,5},{8,6},{9,7},{10,8},{11,9},{12,... | collective-permute-start | bytes 393224 | tf_op jit(solution)/shard_map/ppermute | solution.py:46
  226.7 9.1 %collective-permute-start.27 = (bf16[2,64,512]{2,1,0:T(8,128)(2,1)}, bf16[2,64,512]{2,1,0:T(8,128)(2,1)S(1)}, u32[]{:S(2)}, u32[]{:S(2)}) collective-permute-start(bf16[2,64,512]{2,1,0:T(8,128)(2,1)} %get-tuple-element.101), channel_id=1, source_target_pairs={{0,2},{1,3},{2,4},{3,5},{4,6},{5,7},{6,8},{7,9},{8,10},{9,11},{10,... | collective-permute-start | bytes 393224 | tf_op jit(solution)/shard_map/ppermute | solution.py:46
  231.7 21.7 %collective-permute-start.41 = (bf16[2,192,512]{2,1,0:T(8,128)(2,1)}, bf16[2,192,512]{2,1,0:T(8,128)(2,1)S(1)}, u32[]{:S(2)}, u32[]{:S(2)}) collective-permute-start(bf16[2,192,512]{2,1,0:T(8,128)(2,1)} %get-tuple-element.117), channel_id=1, source_target_pairs={{0,1},{1,2},{2,3},{3,4},{4,5},{5,6},{6,7},{7,8},{8,9},{9,10},{10,1... | collective-permute-start | bytes 1179656 | tf_op jit(solution)/shard_map/ppermute | solution.py:46
  233.0 24.3 %collective-permute-start.32 = (bf16[2,192,512]{2,1,0:T(8,128)(2,1)}, bf16[2,192,512]{2,1,0:T(8,128)(2,1)S(1)}, u32[]{:S(2)}, u32[]{:S(2)}) collective-permute-start(bf16[2,192,512]{2,1,0:T(8,128)(2,1)} %get-tuple-element.107), channel_id=1, source_target_pairs={{1,0},{2,1},{3,2},{4,3},{5,4},{6,5},{7,6},{8,7},{9,8},{10,9},{11,1... | collective-permute-start | bytes 1179656 | tf_op jit(solution)/shard_map/ppermute | solution.py:46
  234.3 14.6 %collective-permute-start.28 = (bf16[2,64,512]{2,1,0:T(8,128)(2,1)}, bf16[2,64,512]{2,1,0:T(8,128)(2,1)S(1)}, u32[]{:S(2)}, u32[]{:S(2)}) collective-permute-start(bf16[2,64,512]{2,1,0:T(8,128)(2,1)} %get-tuple-element.102), channel_id=1, source_target_pairs={{4,0},{5,1},{6,2},{7,3},{8,4},{9,5},{10,6},{11,7},{12,8},{13,9},{1... | collective-permute-start | bytes 393224 | tf_op jit(solution)/shard_map/ppermute | solution.py:46
  235.7 22.9 %collective-permute-start.33 = (bf16[2,192,512]{2,1,0:T(8,128)(2,1)}, bf16[2,192,512]{2,1,0:T(8,128)(2,1)S(1)}, u32[]{:S(2)}, u32[]{:S(2)}) collective-permute-start(bf16[2,192,512]{2,1,0:T(8,128)(2,1)} %get-tuple-element.108), channel_id=1, source_target_pairs={{0,1},{1,2},{2,3},{3,4},{4,5},{5,6},{6,7},{7,8},{8,9},{9,10},{10,1... | collective-permute-start | bytes 1179656 | tf_op jit(solution)/shard_map/ppermute | solution.py:46
  249.0 24.5 %collective-permute-start.24 = (bf16[2,192,512]{2,1,0:T(8,128)(2,1)}, bf16[2,192,512]{2,1,0:T(8,128)(2,1)S(1)}, u32[]{:S(2)}, u32[]{:S(2)}) collective-permute-start(bf16[2,192,512]{2,1,0:T(8,128)(2,1)} %get-tuple-element.98), channel_id=1, source_target_pairs={{1,0},{2,1},{3,2},{4,3},{5,4},{6,5},{7,6},{8,7},{9,8},{10,9},{11,1... | collective-permute-start | bytes 1179656 | tf_op jit(solution)/shard_map/ppermute | solution.py:46
  250.3 23.2 %collective-permute-start.25 = (bf16[2,192,512]{2,1,0:T(8,128)(2,1)}, bf16[2,192,512]{2,1,0:T(8,128)(2,1)S(1)}, u32[]{:S(2)}, u32[]{:S(2)}) collective-permute-start(bf16[2,192,512]{2,1,0:T(8,128)(2,1)} %get-tuple-element.99), channel_id=1, source_target_pairs={{0,1},{1,2},{2,3},{3,4},{4,5},{5,6},{6,7},{7,8},{8,9},{9,10},{10,1... | collective-permute-start | bytes 1179656 | tf_op jit(solution)/shard_map/ppermute | solution.py:46
  253.4 20.0 %collective-permute-start.29 = (bf16[2,64,512]{2,1,0:T(8,128)(2,1)}, bf16[2,64,512]{2,1,0:T(8,128)(2,1)}, u32[]{:S(2)}, u32[]{:S(2)}) collective-permute-start(bf16[2,64,512]{2,1,0:T(8,128)(2,1)} %get-tuple-element.103), channel_id=1, source_target_pairs={{0,4},{1,5},{2,6},{3,7},{4,8},{5,9},{6,10},{7,11},{8,12},{9,13},{1... | collective-permute-start | bytes 393224 | tf_op jit(solution)/shard_map/ppermute | solution.py:46
  257.4 16.0 %collective-permute-start.30 = (bf16[2,64,512]{2,1,0:T(8,128)(2,1)}, bf16[2,64,512]{2,1,0:T(8,128)(2,1)}, u32[]{:S(2)}, u32[]{:S(2)}) collective-permute-start(bf16[2,64,512]{2,1,0:T(8,128)(2,1)} %get-tuple-element.104), channel_id=1, source_target_pairs={{8,0},{9,1},{10,2},{11,3},{12,4},{13,5},{14,6},{15,7},{24,16},{25,... | collective-permute-start | bytes 393224 | tf_op jit(solution)/shard_map/ppermute | solution.py:46
  258.7 14.7 %collective-permute-start.31 = (bf16[2,64,512]{2,1,0:T(8,128)(2,1)}, bf16[2,64,512]{2,1,0:T(8,128)(2,1)}, u32[]{:S(2)}, u32[]{:S(2)}) collective-permute-start(bf16[2,64,512]{2,1,0:T(8,128)(2,1)} %get-tuple-element.105), channel_id=1, source_target_pairs={{0,8},{1,9},{2,10},{3,11},{4,12},{5,13},{6,14},{7,15},{16,24},{17,... | collective-permute-start | bytes 393224 | tf_op jit(solution)/shard_map/ppermute | solution.py:46
  (56 other events, 1285.1 us)

commit v2 on v1

v2 whole, which is shorter than its diff:
```python
import functools
import math

import jax
import jax.numpy as jnp
from jax import lax
from jax.experimental import pallas as pl
from jax.experimental.pallas import tpu as pltpu
from jax.sharding import PartitionSpec as P

HD = 128
BLOCK = 64
LEVELS = 4
KEEP_SCALE = 1.0 / 0.9
ROWS = 128


def logical_right(number, amount):
    return lax.shift_right_logical(number, jnp.full_like(number, amount))


def mixing(number):
    number = number * -1640531535
    number = number ^ logical_right(number, 16)
    number = number * 739982445
    number = number ^ logical_right(number, 15)
    return number


def plan_windows(blocks_dev):
    entries = []
    slot_start = blocks_dev
    for depth_level in range(LEVELS):
        block_count = max(blocks_dev >> depth_level + 1, 1)
        distance = 2**depth_level
        entries.append((distance, slot_start, block_count))
        entries.append((-distance, slot_start + block_count, block_count))
        slot_start = slot_start + 2 * block_count
    return entries


def sender_ids(key_blocks, frame_rank, frames, blocks_dev, shift_by, slot_start, block_count):
    reader = jnp.clip(frame_rank + shift_by, 0, frames - 1)
    reader_row = lax.dynamic_slice_in_dim(key_blocks, reader, 1, 0)[0]
    listed = reader_row[slot_start : slot_start + block_count]
    return jnp.clip(listed - frame_rank * blocks_dev, 0, blocks_dev - 1)


def pack_kernel(counts, ids_ref, k_ref, v_ref, *out_refs):
    at = 0
    for out_ref, count in zip(out_refs, counts):
        for j in range(count):
            start = pl.multiple_of(ids_ref[at] * BLOCK, BLOCK)
            at += 1
            rows = slice(j * BLOCK, (j + 1) * BLOCK)
            out_ref[0, 0, rows, :] = k_ref[pl.ds(start, BLOCK), :]
            out_ref[0, 1, rows, :] = v_ref[pl.ds(start, BLOCK), :]


def contract(a, b, dim_a, dim_b):
    return lax.dot_general(
        a, b, (((dim_a,), (dim_b,)), ((), ())), preferred_element_type=jnp.float32
    )


def fold_rows(x, op):
    total = x[0:8]
    for r in range(8, x.shape[0], 8):
        total = op(total, x[r : r + 8])
    return total


def main_kernel(entries, spans, frames, heads, *refs):
    n_win = len(spans)
    rk_ref, kt_ref, bias_ref, q_ref, k_ref, v_ref, do_ref = refs[:7]
    packed_refs = refs[7 : 7 + n_win]
    outs = refs[7 + n_win :]
    att_ref, dq_ref, own_ref = outs[:3]
    ret_refs = outs[3 : 3 + n_win]
    scratch = outs[3 + n_win :]
    kall, vall, s_ref, dp_ref, pd_ref, ds_ref, gk_ref, gv_ref = scratch[:8]
    win_refs = scratch[8 : 8 + n_win]
    back_refs = scratch[8 + n_win : 8 + 2 * n_win]
    fetch_send, fetch_recv, back_send, back_recv = scratch[8 + 2 * n_win :]
    tok = q_ref.shape[0]
    slots = kall.shape[0]
    score_scale = 1.0 / math.sqrt(HD)
    exp_scale = score_scale * math.log2(math.e)
    steps = slots // ROWS
    tiles = tok // 128
    head = pl.program_id(0)
    rank = lax.axis_index("frame")
    distances = [entry[0] for entry in entries]

    def present(other):
        return jnp.logical_and(other >= 0, other < frames)

    def fetch(w, h):
        return pltpu.make_async_remote_copy(
            src_ref=packed_refs[w].at[h], dst_ref=win_refs[w].at[h],
            send_sem=fetch_send.at[w, h], recv_sem=fetch_recv.at[w, h],
            device_id={"frame": lax.rem(rank + distances[w] + frames, frames)}, device_id_type=pl.DeviceIdType.MESH,
        )

    def give_back(w, h):
        return pltpu.make_async_remote_copy(
            src_ref=back_refs[w].at[h], dst_ref=ret_refs[w].at[h],
            send_sem=back_send.at[w, h], recv_sem=back_recv.at[w, h],
            device_id={"frame": lax.rem(rank - distances[w] + frames, frames)}, device_id_type=pl.DeviceIdType.MESH,
        )

    @pl.when(head == 0)
    def _():
        barrier = pltpu.get_barrier_semaphore()
        for d in distances:
            @pl.when(present(rank + d))
            def _(d=d):
                pl.semaphore_signal(
                    barrier, inc=1, device_id={"frame": rank + d},
                    device_id_type=pl.DeviceIdType.MESH,
                )
        peers = jnp.int32(0)
        for d in distances:
            peers = peers + present(rank + d).astype(jnp.int32)
        pl.semaphore_wait(barrier, peers)

        def send_head(h, _):
            for w, d in enumerate(distances):
                @pl.when(present(rank + d))
                def _(w=w):
                    fetch(w, h).start()
            return 0

        lax.fori_loop(0, heads, send_head, 0)

    kall[0:tok, :] = k_ref[...]
    vall[0:tok, :] = v_ref[...]
    for w, (lo, hi) in enumerate(spans):
        @pl.when(present(rank - distances[w]))
        def _(w=w, lo=lo, hi=hi):
            fetch(w, head).wait_recv()
            kall[lo:hi, :] = win_refs[w][head, 0]
            vall[lo:hi, :] = win_refs[w][head, 1]

        @pl.when(jnp.logical_not(present(rank - distances[w])))
        def _(lo=lo, hi=hi):
            kall[lo:hi, :] = jnp.zeros((hi - lo, HD), jnp.bfloat16)
            vall[lo:hi, :] = jnp.zeros((hi - lo, HD), jnp.bfloat16)

    def rows_of(j):
        return pl.ds(pl.multiple_of(j * ROWS, ROWS), ROWS)

    def pass_a(j, top):
        rows = rows_of(j)
        raw = contract(kall[rows, :], q_ref[...], 1, 1)
        bias = bias_ref[rows, :]
        new_top = []
        for t in range(tiles):
            lanes = slice(t * 128, (t + 1) * 128)
            s = raw[:, lanes] + bias
            s_ref[rows, lanes] = s
            new_top.append(jnp.maximum(top[t], fold_rows(s, jnp.maximum)))
        return tuple(new_top)

    top = lax.fori_loop(
        0, steps, pass_a, tuple(jnp.full((8, 128), -jnp.inf, jnp.float32) for _ in range(tiles))
    )
    top = [jnp.max(t, axis=0, keepdims=True) for t in top]
    head_term = head * 977
    row_keys = [rk_ref[:, t * 128 : (t + 1) * 128] for t in range(tiles)]

    def pass_b(j, sums):
        rows = rows_of(j)
        grads = contract(vall[rows, :], do_ref[...], 1, 1)
        token_term = kt_ref[rows, :] + head_term
        new_sums = []
        for t in range(tiles):
            lanes = slice(t * 128, (t + 1) * 128)
            e = jnp.exp2((s_ref[rows, lanes] - top[t]) * exp_scale)
            x = token_term ^ row_keys[t]
            x = x * -1640531535
            x = x ^ logical_right(x, 16)
            x = x * 739982445
            x = x ^ logical_right(x, 15)
            keep = (x & (1023 << 16)) >= (102 << 16)
            dp = grads[:, lanes]
            dp_ref[rows, lanes] = dp
            s_ref[rows, lanes] = jnp.where(keep, e, -e)
            kept = jnp.where(keep, e * dp, 0.0)
            new_sums.append(sums[2 * t] + fold_rows(e, jnp.add))
            new_sums.append(sums[2 * t + 1] + fold_rows(kept, jnp.add))
        return tuple(new_sums)

    sums = lax.fori_loop(
        0, steps, pass_b, tuple(jnp.zeros((8, 128), jnp.float32) for _ in range(2 * tiles))
    )
    sums = [jnp.sum(x, axis=0, keepdims=True) for x in sums]
    inv = [KEEP_SCALE / sums[2 * t] for t in range(tiles)]
    inv_scaled = [x * score_scale for x in inv]
    delta = [sums[2 * t + 1] * inv[t] * (inv_scaled[t] / KEEP_SCALE) for t in range(tiles)]

    def pass_c(j, _):
        rows = rows_of(j)
        for t in range(tiles):
            lanes = slice(t * 128, (t + 1) * 128)
            es = s_ref[rows, lanes]
            kept = jnp.maximum(es, 0.0)
            pd = kept * inv[t]
            ds = kept * inv_scaled[t] * dp_ref[rows, lanes] - jnp.abs(es) * delta[t]
            pd_ref[rows, lanes] = pd.astype(jnp.bfloat16)
            ds_ref[rows, lanes] = ds.astype(jnp.bfloat16)
        gk_ref[rows, :] = contract(ds_ref[rows, :], q_ref[...], 1, 0)
        gv_ref[rows, :] = contract(pd_ref[rows, :], do_ref[...], 1, 0)
        return 0

    lax.fori_loop(0, steps, pass_c, 0)
    own_ref[0] = gk_ref[0:tok, :]
    own_ref[1] = gv_ref[0:tok, :]
    for back_ref, (lo, hi) in zip(back_refs, spans):
        back_ref[head, 0] = gk_ref[lo:hi, :].astype(jnp.bfloat16)
        back_ref[head, 1] = gv_ref[lo:hi, :].astype(jnp.bfloat16)
    att_ref[...] = contract(pd_ref[...], vall[...], 0, 0).astype(jnp.bfloat16)
    dq_ref[...] = contract(ds_ref[...], kall[...], 0, 0).astype(jnp.bfloat16)
    for w, d in enumerate(distances):
        @pl.when(present(rank - d))
        def _(w=w):
            give_back(w, head).start()

    @pl.when(head == heads - 1)
    def _():
        def drain(h, _):
            for w, d in enumerate(distances):
                @pl.when(present(rank + d))
                def _(w=w):
                    fetch(w, h).wait_send()
                    give_back(w, h).wait_recv()

                @pl.when(present(rank - d))
                def _(w=w):
                    give_back(w, h).wait_send()
            return 0

        lax.fori_loop(0, heads, drain, 0)


def finish_kernel(counts, ids_ref, live_ref, own_ref, *refs):
    ret_refs = refs[: len(counts)]
    kg_ref, vg_ref, acc = refs[len(counts) :]
    acc[...] = own_ref[...]
    at = 0
    for w, (ret_ref, count) in enumerate(zip(ret_refs, counts)):
        @pl.when(live_ref[w] > 0)
        def _(ret_ref=ret_ref, count=count, at=at):
            for j in range(count):
                rows = pl.ds(pl.multiple_of(ids_ref[at + j] * BLOCK, BLOCK), BLOCK)
                part = ret_ref[0, :, j * BLOCK : (j + 1) * BLOCK, :]
                acc[:, rows, :] += part.astype(jnp.float32)
        at += count
    kg_ref[...] = acc[0].astype(jnp.bfloat16)
    vg_ref[...] = acc[1].astype(jnp.bfloat16)


def local(queries, keys, values, out_grad, key_blocks, seed_offsets, dropout_seed):
    tok, width = queries.shape
    blocks_dev = tok // BLOCK
    heads = width // HD
    frames = lax.axis_size("frame")
    frame_rank = lax.axis_index("frame")
    entries = plan_windows(blocks_dev)
    counts = [count for _, _, count in entries]
    spans = [(start * BLOCK, (start + count) * BLOCK) for _, start, count in entries]
    slots = key_blocks.shape[1] * BLOCK
    ids = jnp.concatenate(
        [sender_ids(key_blocks, frame_rank, frames, blocks_dev, *entry) for entry in entries]
    )
    listed = lax.dynamic_slice_in_dim(key_blocks, frame_rank, 1, 0)[0]
    alive = listed >= 0
    tokens = (jnp.where(alive, listed, 0)[:, None] * BLOCK + jnp.arange(BLOCK, dtype=jnp.int32)).reshape(-1)
    token_terms = jnp.broadcast_to((tokens * 40503)[:, None], (slots, 128))
    bias = jnp.where(jnp.repeat(alive, BLOCK), 0.0, -jnp.inf).astype(jnp.float32)
    bias = jnp.broadcast_to(bias[:, None], (slots, 128))
    query_tokens = frame_rank * tok + jnp.arange(tok, dtype=jnp.int32)
    row_keys = mixing(dropout_seed[0] + jnp.repeat(seed_offsets, BLOCK) + query_tokens * 7919)[None, :]

    bf16, f32 = jnp.bfloat16, jnp.float32
    smem = pl.BlockSpec(memory_space=pltpu.SMEM)
    anyspec = pl.BlockSpec(memory_space=pl.ANY)
    win_shapes = [jax.ShapeDtypeStruct((heads, 2, n * BLOCK, HD), bf16) for n in counts]
    win_specs = [pl.BlockSpec((1, 2, n * BLOCK, HD), lambda h: (h, 0, 0, 0)) for n in counts]
    full = jax.ShapeDtypeStruct((tok, width), bf16)
    column = pl.BlockSpec((tok, HD), lambda h: (0, h))
    own_spec = pl.BlockSpec((2, tok, HD), lambda h: (0, 0, h))
    table = pl.BlockSpec((slots, 128), lambda h: (0, 0))
    n_win = len(entries)
    reach = frame_rank + jnp.array([entry[0] for entry in entries], jnp.int32)
    live = jnp.logical_and(reach >= 0, reach < frames).astype(jnp.int32)

    packed = pl.pallas_call(
        functools.partial(pack_kernel, counts),
        grid=(heads,),
        in_specs=[smem, column, column],
        out_specs=win_specs,
        out_shape=win_shapes,
        name="pack",
    )(ids, keys, values)
    result = pl.pallas_call(
        functools.partial(main_kernel, entries, spans, frames, heads),
        grid=(heads,),
        in_specs=[
            pl.BlockSpec((1, tok), lambda h: (0, 0)), table, table,
            column, column, column, column, *([anyspec] * n_win),
        ],
        out_specs=[column, column, own_spec, *([anyspec] * n_win)],
        out_shape=[full, full, jax.ShapeDtypeStruct((2, tok, width), f32), *win_shapes],
        scratch_shapes=[
            pltpu.VMEM((slots, HD), bf16),
            pltpu.VMEM((slots, HD), bf16),
            pltpu.VMEM((slots, tok), f32),
            pltpu.VMEM((slots, tok), f32),
            pltpu.VMEM((slots, tok), bf16),
            pltpu.VMEM((slots, tok), bf16),
            pltpu.VMEM((slots, HD), f32),
            pltpu.VMEM((slots, HD), f32),
            *[pltpu.VMEM(shape.shape, bf16) for shape in win_shapes],
            *[pltpu.VMEM(shape.shape, bf16) for shape in win_shapes],
            *([pltpu.SemaphoreType.DMA((n_win, heads))] * 4),
        ],
        compiler_params=pltpu.CompilerParams(
            dimension_semantics=("arbitrary",), collective_id=0, has_side_effects=True
        ),
        name="attend",
    )(row_keys, token_terms, bias, queries, keys, values, out_grad, *packed)
    grads = pl.pallas_call(
        functools.partial(finish_kernel, counts),
        grid=(heads,),
        in_specs=[smem, smem, own_spec, *win_specs],
        out_specs=[column, column],
        out_shape=[full, full],
        scratch_shapes=[pltpu.VMEM((2, tok, HD), f32)],
        name="finish",
    )(ids, live, result[2], *result[3:])
    return (result[0], result[1], grads[0], grads[1])


def solution(mesh):
    rows = P(("rep", "frame"), None)
    return jax.shard_map(
        local,
        mesh=mesh,
        in_specs=(rows, rows, rows, rows, P("rep", None), P(("rep", "frame")), P("rep")),
        out_specs=(rows, rows, rows, rows),
        check_vma=False,
    )
```

time: 280 us -> 144 us (0.51)
  starting transfers between devices: 141 us -> 0 us
  Pallas kernels: 103 us -> 123 us
  waiting for transfers between devices: 14.9 us -> 0 us
    ppermute x48 -> x0, starting transfers between devices: 141 us -> none  [shift(): return lax.ppermute(value, 'frame', pairs)]
    pallas_call x9 -> x3, Pallas kernels: 103 us -> 123 us  [the longest x1 106 us: local(): pl.pallas_call(functools.partial(main_kernel, entries, spans, frames, hea...]
    ppermute x48 -> x0, waiting for transfers between devices: 14.9 us -> none  [shift(): return lax.ppermute(value, 'frame', pairs)]
  transfers between devices with their start and end apart: 48 -> 0, of which waited for: 3 -> 0; matrix products, arithmetic and copies ran while one was open for 2% -> 0% of each run, Pallas kernels for 35% -> 0%
where the time goes in v2:
time: 144 us; the launch traced here: 143 us
  Pallas kernels  123 us (85%)
  local copies, waits for them, and re-layouts  10.2 us (7%)
  between operations  5.28 us (4%)
  other arithmetic  4.02 us (3%)
    pallas_call x1, Pallas kernels, local(): pl.pallas_call(functools.partial(main_kernel, entries, spans, frames, hea...  106 us
    pallas_call x1, Pallas kernels, local(): pl.pallas_call(functools.partial(finish_kernel, counts), grid=(heads,), i...  9.65 us
    pallas_call x1, Pallas kernels, local(): pl.pallas_call(functools.partial(pack_kernel, counts), grid=(heads,), in_...  8.22 us
    slice x6, local copies, waits for them, and re-layouts, sender_ids(): listed = reader_row[slot_start:slot_start + block_count]  3.49 us

profile of v2, /device:TPU:0, one launch (start us, length us, event | category | flops | bytes accessed | tf_op | source)
XLA Modules:
  0.0 143.0 jit_solution(8597220288144149285)
XLA Ops:
  1.3 0.7 broadcast_add_fusion
  2.0 1.2 and_convert_fusion.live_ref
  3.2 1.0 constant_dynamic-slice_fusion
  4.2 0.6 slice.54
  5.4 0.6 slice.46
  6.6 0.6 slice.48
  7.9 0.6 slice.50
  9.1 0.6 slice.52
  10.3 0.6 slice.56
  11.6 0.7 compare_select_fusion
  12.3 0.7 fusion.1
  13.0 0.1 clamp_bitcast_fusion
  13.0 0.6 concatenate.3.ids_ref
  13.7 0.1 broadcast_in_dim.37
  13.7 0.1 add.102
  13.8 0.6 shift-right-logical_xor_fusion.refs_0_
  14.4 0.1 add_multiply_fusion
  14.5 0.1 mul.83
  14.6 0.1 broadcast_in_dim.43
  14.6 0.1 select_n.34
  14.7 1.0 broadcast_in_dim.44.refs_2_
  15.7 1.0 broadcast_in_dim.40.refs_1_
  16.8 8.2 %pack.1 = (bf16[12,2,192,128]{3,2,1,0:T(8,128)(2,1)}, bf16[12,2,192,128]{3,2,1,0:T(8,128)(2,1)}, bf16[12,2,64,128]{3,2,1,0:T(8,128)(2,1)}, bf16[12,2,64,128]{3,2...) custom-call(s32[12]{0:T(128)} %concatenate.3.ids_ref, ...), custom_call_target="tpu_custom_call" | custom-call | tf_op jit(solution)/shard_map/pack/pallas_call | solution.py:298
  25.0 105.6 %attend.1 = (bf16[384,1536]{1,0:T(8,128)(2,1)}, bf16[384,1536]{1,0:T(8,128)(2,1)}, f32[2,384,1536]{2,1,0:T(8,128)}, bf16[12,2,192,128]{3,2,1,0:T(8,128)(2,1)}, b...) custom-call(s32[1,384]{1,0:T(1,128)} %shift-right-logical_xor_fusion, ...), custom_call_target="tpu_custom_call" | custom-call | tf_op jit(solution)/shard_map/attend/pallas_call | solution.py:306
  130.6 0.0 copy-start.1
  130.6 9.7 %finish.1 = (bf16[384,1536]{1,0:T(8,128)(2,1)}, bf16[384,1536]{1,0:T(8,128)(2,1)}) custom-call(s32[12]{0:T(128)} %concatenate.3.ids_ref, s32[8]{0:T(128)} %and_convert_fusion.live_ref, f32[2,384,1536]{2,1,0:T(8,128)} %get-tuple-element.35.own_ref, bf16[12,2,192,128]{3,2,1,0:T(8,128)(2,1)} %get-tuple-element.36.refs_0_, ...), custom_call_target="tpu_custom_call" | custom-call | tf_op jit(solution)/shard_map/finish/pallas_call | solution.py:333
  140.2 0.0 copy-done.1
  140.3 0.0 copy-start
  140.3 1.0 copy.15
  141.3 0.7 copy-done
  141.9 1.0 copy.16
Async XLA Ops:
  130.6 9.7 %copy-start.1 = (bf16[384,1536]{1,0:T(8,128)(2,1)S(1)}, bf16[384,1536]{1,0:T(8,128)(2,1)}, u32[]{:S(2)}) copy-start(bf16[384,1536]{1,0:T(8,128)(2,1)} %get-tuple-element.60) | copy-start | bytes 3538948
  140.3 1.7 %copy-start = (bf16[384,1536]{1,0:T(8,128)(2,1)S(1)}, bf16[384,1536]{1,0:T(8,128)(2,1)}, u32[]{:S(2)}) copy-start(bf16[384,1536]{1,0:T(8,128)(2,1)} %get-tuple-element.61) | copy-start | bytes 3538948
